TPU v7x, 256 devices: a whole 4x4x8 slice. The times are simulated.
256 devices in a mesh: seq: 128 (over x_lo, z, y, core), mp: 2 (over x_hi).
Axes of the slice: x: 4 (x_hi: 2, x_lo: 2; x = x_hi * 2 + x_lo), y: 4, z: 8, core: 2. Of those that a mesh axis runs over, the one named last changes fastest.
Arguments:
- patches: bfloat16 [32768, 64], P('seq'), may hold values from -6 to 6
- clip_shape: int32 [64, 3], replicated, may hold values from 1 to 16, as said below
- shard_counts: int32 [128], replicated, may hold values from 1 to 256, as said below
- patch_weight: bfloat16 [64, 2560], P(None, 'mp'), may hold values from -3 to 3
- patch_bias: float32 [2560], P('mp'), may hold values from -6 to 6
- time_mod: float32 [64, 2, 2560], P(None, None, 'mp'), may hold values from -6 to 6
- block_mod: float32 [2, 2560], P(None, 'mp'), may hold values from -4 to 4
- w_query: bfloat16 [2560, 2560], P('seq', 'mp'), may hold values from -0.47434165 to 0.47434165
- query_bias: float32 [2560], P('mp'), may hold values from -4 to 4
- w_keyvalue: bfloat16 [2560, 5120], P('seq', 'mp'), may hold values from -0.47434165 to 0.47434165
- keyvalue_bias: float32 [5120], P('mp'), may hold values from -6 to 6
- norm_gain: float32 [2, 2560], P(None, 'mp'), may hold values from 1 to 2
Outputs:
- attention: bfloat16 [32768, 2560], P('seq', 'mp')
Inputs may be any that keep to these rules, and one draw needn't show every extreme that they name: `clip_shape`: clip c lies on shards 2 c to 2 c + 1. Frames run from 1 to 2, patch rows from 8 to 16, patch columns from 8 to 16; some clip has 2 frames of 16 by 16 patches. `shard_counts`: the counts of clip c's 2 shards add up to the product of clip_shape[c].
All inputs are finite; a program needn't handle non-finite values.
Results may differ from a plain program's by a relative error of at most 0.0063.
Values may be sent and summed in bfloat16 or wider, within the bound.
A program may use at most 128 MiB of HBM per device.

v0:
```python
import math

import jax
import jax.numpy as jnp
from jax import lax
from jax.sharding import PartitionSpec as P

D = 2560
HEADS = 20
HD = 128
GROUP = 2


EPSILON = 1e-06


def partner_2(value, axis, apart):
    mask = 2**apart
    pairs = [(source, source ^ mask) for source in range(lax.axis_size(axis))]
    return lax.ppermute(value, axis, pairs)


def token_places(group_counts, member_ids, slot_ids, shape_row):
    before = jnp.cumsum(group_counts) - group_counts
    lookup = jnp.arange(GROUP, dtype=jnp.int32)[None, :] == member_ids[:, None]
    offset = jnp.sum(jnp.where(lookup, before[None, :], 0), axis=1)
    holding = jnp.sum(jnp.where(lookup, group_counts[None, :], 0), axis=1)
    position = offset + slot_ids
    plane_size = shape_row[1] * shape_row[2]
    frame_pos = position // plane_size
    row_pos = position // shape_row[2] % shape_row[1]
    col_pos = position % shape_row[2]
    return (slot_ids < holding, frame_pos, row_pos, col_pos)


def rotary_tables(frame_pos, row_pos, col_pos):
    other_pairs = HD // 6
    frame_pairs = HD // 2 - 2 * other_pairs
    pair_id = jnp.arange(HD, dtype=jnp.int32) // 2
    in_frame = pair_id < frame_pairs
    in_row = jnp.logical_and(pair_id >= frame_pairs, pair_id < frame_pairs + other_pairs)
    within = jnp.where(
        in_frame,
        pair_id,
        jnp.where(in_row, pair_id - frame_pairs, pair_id - frame_pairs - other_pairs),
    ).astype(jnp.float32)
    axis_span = jnp.where(in_frame, 2.0 * frame_pairs, 2.0 * other_pairs).astype(jnp.float32)
    inverse = jnp.exp(-(2.0 * within / axis_span) * math.log(10000.0))
    position = jnp.where(
        in_frame[None, :],
        frame_pos[:, None],
        jnp.where(in_row[None, :], row_pos[:, None], col_pos[:, None]),
    ).astype(jnp.float32)
    angles = position * inverse[None, :]
    return (jnp.cos(angles), jnp.sin(angles))


def rotate_pairs(values, cosine_table, sine_table):
    parity = jnp.arange(HD, dtype=jnp.int32) % 2 == 0
    partner = jnp.where(parity, -jnp.roll(values, -1, axis=-1), jnp.roll(values, 1, axis=-1))
    return values * cosine_table[:, None, :] + partner * sine_table[:, None, :]


def modulate_rows(embedded, row_sums, squares, modulation):
    average = row_sums / D
    variance = squares / D - average * average
    normed = (embedded - average[:, None]) * lax.rsqrt(variance[:, None] + EPSILON)
    return (normed * (1.0 + modulation[1]) + modulation[0]).astype(jnp.bfloat16)


def finish_heads(raw_rows, squares, scale_gain, cosine_table, sine_table):
    normed = raw_rows * lax.rsqrt(squares[:, None] / (HEADS * HD) + EPSILON) * scale_gain
    return rotate_pairs(normed.reshape(raw_rows.shape[0], -1, HD), cosine_table, sine_table).astype(
        jnp.bfloat16
    )


def contract(left_rows, pieces):
    return jnp.dot(left_rows, pieces, preferred_element_type=jnp.float32)


def split_pairs(pair_acc, keyvalue_bias, heads_here):
    tokens = pair_acc.shape[0]
    pair_raw = (pair_acc + keyvalue_bias).reshape(tokens, heads_here, 2, HD)
    key_raw = pair_raw[:, :, 0].reshape(tokens, heads_here * HD)
    value_rows = pair_raw[:, :, 1].reshape(tokens, heads_here * HD).astype(jnp.bfloat16)
    return (key_raw, value_rows)


def count_of(group_counts, source):
    return jnp.sum(jnp.where(jnp.arange(GROUP, dtype=jnp.int32) == source, group_counts, 0))


def gather_group(key_rows, value_rows, member):
    tokens = value_rows.shape[0]
    blocks = jnp.stack([key_rows.reshape(tokens, -1), value_rows])
    sources = [member]
    partner = partner_2(blocks, "seq", 0)
    blocks = jnp.concatenate([blocks, partner], axis=1)
    sources = sources + [jnp.bitwise_xor(source, 1 << 0) for source in sources]
    return (blocks, sources)


def attend_rows(queries, all_keys, all_values, key_valid):
    scores = jnp.einsum(
        "qhd,khd->hqk", queries, all_keys, preferred_element_type=jnp.float32
    ) * HD ** (-0.5)
    weights = jnp.where(key_valid[None, None, :], jnp.exp(scores), 0.0)
    totals = jnp.sum(weights, axis=-1)
    numerator = jnp.einsum(
        "hqk,khd->qhd", weights.astype(jnp.bfloat16), all_values, preferred_element_type=jnp.float32
    )
    return numerator / jnp.transpose(totals)[:, :, None]


def shards(
    patches,
    clip_shape,
    shard_counts,
    patch_weight,
    patch_bias,
    time_mod,
    block_mod,
    w_query,
    query_bias,
    w_keyvalue,
    keyvalue_bias,
    norm_gain,
):
    tokens = patches.shape[0]
    heads_here = w_query.shape[1] // HD
    seq_index = lax.axis_index("seq")
    clip_id = seq_index // GROUP
    member = seq_index % GROUP
    group_counts = lax.dynamic_slice_in_dim(shard_counts, clip_id * GROUP, GROUP, 0)
    shape_row = lax.dynamic_index_in_dim(clip_shape, clip_id, 0, keepdims=False)
    slot_ids = jnp.arange(tokens, dtype=jnp.int32)
    is_valid, frame_pos, row_pos, col_pos = token_places(
        group_counts, jnp.full((tokens,), member, jnp.int32), slot_ids, shape_row
    )
    modulation = lax.dynamic_index_in_dim(time_mod, clip_id, 0, keepdims=False) + block_mod
    embedded = jnp.dot(patches, patch_weight, preferred_element_type=jnp.float32) + patch_bias
    row_sums, squares = lax.psum(
        (jnp.sum(embedded, axis=1), jnp.sum(embedded * embedded, axis=1)), "mp"
    )
    half_rows = modulate_rows(embedded, row_sums, squares, modulation)
    hidden = lax.all_gather(half_rows, "mp", axis=1, tiled=True)
    cosine_table, sine_table = rotary_tables(frame_pos, row_pos, col_pos)
    query_acc = contract(hidden, lax.all_gather(w_query, "seq", axis=0, tiled=True))
    pair_acc = contract(hidden, lax.all_gather(w_keyvalue, "seq", axis=0, tiled=True))
    query_raw = query_acc + query_bias
    key_raw, value_rows = split_pairs(pair_acc, keyvalue_bias, heads_here)
    query_squares, key_squares = lax.psum(
        (jnp.sum(query_raw * query_raw, axis=1), jnp.sum(key_raw * key_raw, axis=1)), "mp"
    )
    queries = finish_heads(query_raw, query_squares, norm_gain[0], cosine_table, sine_table)
    key_rows = finish_heads(key_raw, key_squares, norm_gain[1], cosine_table, sine_table)
    blocks, sources = gather_group(key_rows, value_rows, member)
    key_valid = jnp.concatenate([slot_ids < count_of(group_counts, source) for source in sources])
    all_keys = blocks[0].reshape(-1, heads_here, HD)
    all_values = blocks[1].reshape(-1, heads_here, HD)
    result = attend_rows(queries, all_keys, all_values, key_valid)
    result = jnp.where(is_valid[:, None, None], result, 0.0)
    return result.reshape(tokens, heads_here * HD).astype(jnp.bfloat16)


def solution(mesh):
    return jax.shard_map(
        shards,
        mesh=mesh,
        in_specs=(
            P("seq", None),
            P(),
            P(),
            P(None, "mp"),
            P("mp"),
            P(None, None, "mp"),
            P(None, "mp"),
            P("seq", "mp"),
            P("mp"),
            P("seq", "mp"),
            P("mp"),
            P(None, "mp"),
        ),
        out_specs=P("seq", "mp"),
        check_vma=False,
    )
```

profile of v0, /device:TPU:1, one launch (start us, length us, event | category | flops | bytes accessed | tf_op | source)
XLA Modules:
  0.0 569.0 jit_solution(236258735546962702)
XLA Ops:
  7.5 1.2 fusion.33
  8.7 5.9 %all-reduce.1 = (f32[256]{0:T(256)S(1)}, f32[256]{0:T(256)S(1)}) all-reduce(f32[256]{0:T(256)S(1)} %get-tuple-element.6, f32[256]{0:T(256)S(1)} %get-tuple-element.5), channel_id=1, replica_groups=mesh['seq'=128,'mp'=2] {'mp'}, use_global_device_ids=true, to_apply=%region_4.5 | all-reduce | flops 512 | bytes 4096 | tf_op jit(solution)/shard_map/psum | solution.py:143
  15.4 1.1 add_convert_fusion
  23.3 1.3 iota_compare_fusion
  26.2 205.1 %all-gather.10.cloned.1.call-done = bf16[128,20,1280]{2,1,0:T(8,128)(2,1)} async-done(((bf16[1,20,1280]{2,1,0:T(8,128)(2,1)}), bf16[128,20,1280]{2,1,0:T(8,128)(2,1)}) %all-gather.10.cloned.1.call-update) | async-done | bytes 6553616 | tf_op jit(solution)/shard_map/all_gather | solution.py:149
  231.3 10.6 %reshape.424 = bf16[2560,1280]{1,0:T(8,128)(2,1)} reshape(bf16[128,20,1280]{2,1,0:T(8,128)(2,1)} %all-gather.10.cloned.1.call-done) | data formatting | bytes 13107200
  241.9 20.6 %all-gather.6.cloned.1.call-done = bf16[256,2560]{1,0:T(8,128)(2,1)} async-done(((bf16[256,1280]{1,0:T(8,128)(2,1)}), bf16[256,2560]{1,0:T(8,128)(2,1)}) %all-gather.6.cloned.1.call-update) | async-done | bytes 1310736 | tf_op jit(solution)/shard_map/all_gather | solution.py:147
  262.6 6.2 %multiply_reduce_fusion = (f32[256]{0:T(256)S(1)}, f32[256,1280]{1,0:T(8,128)}) fusion(f32[1280]{0:T(1024)S(1)} %copy-done.12, bf16[256,2560]{1,0:T(8,128)(2,1)} %all-gather.6.cloned.1.call-done, bf16[2560,1280]{1,0:T(8,128)(2,1)} %reshape.424), kind=kOutput, calls=%fused_computation.31 | convolution fusion | flops 1678704384 | bytes 9181184 | tf_op jit(solution)/shard_map/dot_general | solution.py:79
  268.7 222.9 %all-gather.8.cloned.1.call-done = bf16[128,20,2560]{2,1,0:T(8,128)(2,1)} async-done(((bf16[1,20,2560]{2,1,0:T(8,128)(2,1)}), bf16[128,20,2560]{2,1,0:T(8,128)(2,1)}) %all-gather.8.cloned.1.call-update) | async-done | bytes 13107216 | tf_op jit(solution)/shard_map/all_gather | solution.py:150
  491.7 18.0 %reshape.422 = bf16[2560,2560]{1,0:T(8,128)(2,1)} reshape(bf16[128,20,2560]{2,1,0:T(8,128)(2,1)} %all-gather.8.cloned.1.call-done) | data formatting | bytes 26214400
  509.7 7.0 %convolution_add_fusion = f32[256,2560]{1,0:T(8,128)S(1)} fusion(bf16[256,2560]{1,0:T(8,128)(2,1)} %all-gather.6.cloned.1.call-done, bf16[2560,2560]{1,0:T(8,128)(2,1)} %reshape.422, f32[2560]{0:T(1024)S(1)} %copy-done.11), kind=kOutput, calls=%fused_computation.3 | convolution fusion | flops 3356098560 | bytes 17049600 | tf_op jit(solution)/shard_map/dot_general | solution.py:79
  516.7 2.8 reshape.417
  519.5 2.6 slice.84
  522.3 5.5 all-reduce
  528.0 1.5 fusion.37
  529.5 2.0 fusion.38
  531.5 2.1 copy.42
  533.6 4.3 slice.89
  538.0 1.5 maximum_negate_fusion
  539.5 2.9 copy.43
  542.3 1.5 pad_maximum_fusion.1
  543.9 2.9 copy.44
  546.8 1.0 copy.54
  547.7 2.5 fusion.15
  550.3 1.2 pad_maximum_fusion.2
  551.5 2.3 collective-permute-start
  553.7 1.3 multiply_multiply_fusion
  555.0 1.7 copy.46
  557.0 1.5 pad_maximum_fusion
  558.7 1.6 fusion
  560.4 1.0 select_convert_fusion
  561.4 1.1 copy.49
  (58 shorter events, 6.4 us)
Async XLA Ops:
  6.5 0.9 copy-start
  6.5 8.0 %copy-start.7 = (f32[2,1280]{1,0:T(2,128)S(1)}, f32[2,1280]{1,0:T(2,128)}, u32[]{:S(2)}) copy-start(f32[2,1280]{1,0:T(2,128)} %param.18) | copy-start | bytes 30724
  6.5 224.8 %all-gather.10.cloned.1.call-start = ((), (), s32[]{:S(2)}) async-start(), calls=%async_computation.2 | async-start | bytes 7925760 | tf_op jit(solution)/shard_map/all_gather | solution.py:149
  7.3 255.3 %all-gather.6.cloned.1.call-start = ((), (), s32[]{:S(2)}) async-start(), calls=%async_computation | async-start | bytes 1966080 | tf_op jit(solution)/shard_map/all_gather | solution.py:147
  15.3 1.9 copy-start.9
  15.3 5.7 %copy-start.10 = (s32[128]{0:T(128)S(1)}, s32[128]{0:T(128)}, u32[]{:S(2)}) copy-start(s32[128]{0:T(128)} %param.14) | copy-start | bytes 1540
  15.4 9.2 %copy-start.8 = (f32[2,1280]{1,0:T(2,128)S(1)}, f32[2,1280]{1,0:T(2,128)}, u32[]{:S(2)}) copy-start(f32[2,1280]{1,0:T(2,128)} %param.23) | copy-start | bytes 30724
  16.5 475.1 %all-gather.8.cloned.1.call-start = ((), (), s32[]{:S(2)}) async-start(), calls=%async_computation.1 | async-start | bytes 15851520 | tf_op jit(solution)/shard_map/all_gather | solution.py:150
  26.1 236.4 %copy-start.12 = (f32[1280]{0:T(1024)S(1)}, f32[1280]{0:T(1024)}, u32[]{:S(2)}) copy-start(f32[1280]{0:T(1024)} %param.20) | copy-start | bytes 15364
  268.7 241.0 %copy-start.11 = (f32[2560]{0:T(1024)S(1)}, f32[2560]{0:T(1024)}, u32[]{:S(2)}) copy-start(f32[2560]{0:T(1024)} %param.22) | copy-start | bytes 30724
  533.6 4.3 copy-start.4
  533.6 4.3 copy-start.5
  539.5 2.9 copy-start.2
  543.9 2.9 copy-start.3
  550.3 3.5 copy-start.6
  551.5 5.6 collective-permute-start
  560.3 2.1 copy-start.1
Sparse Core Ops, SparseCore 0:
  9.2 222.0 all-gather.9
  233.1 29.4 all-gather.5
  264.4 227.1 all-gather.7
where the time goes:
time: 570 us; the launch traced here: 569 us
  waiting for transfers between devices  450 us (79%)
  local copies, waits for them, and re-layouts  55 us (10%)
  between operations  17.7 us (3%)
  matrix products  17.1 us (3%)
  other arithmetic  15.4 us (3%)
  blocking collectives  11.3 us (2%)
    all_gather x1, waiting for transfers between devices, shards(): lax.all_gather(w_keyvalue, 'seq', axis=0, tiled=True)  223 us
    all_gather x1, waiting for transfers between devices, shards(): lax.all_gather(w_query, 'seq', axis=0, tiled=True)  205 us
    unnamed x29, local copies, waits for them, and re-layouts  29.8 us
    all_gather x1, waiting for transfers between devices, shards(): hidden = lax.all_gather(half_rows, 'mp', axis=1, tiled=True)  20.6 us
    dot_general x2, matrix products, contract(): return jnp.dot(left_rows, pieces, preferred_element_type=jnp.float32)  13.2 us
  transfers between devices with their start and end apart: 4, of which 3 were waited for; matrix products, arithmetic and copies ran while one was open for 5% of the time, Pallas kernels for 0%

commit v1 on v0

v1 whole, which is shorter than its diff:
```python
import functools
import math

import jax
import jax.numpy as jnp
from jax import lax
from jax.experimental import pallas as pl
from jax.experimental.pallas import tpu as pltpu
from jax.sharding import PartitionSpec as P

D = 2560
HALF = D // 2
HEADS = 20
HD = 128
CIN = 64
TOK = 256
PLANE = 32
COLS = 16
ROWS = 4
UNITS = 30
OWN = 5
BLOCK = 80
EPSILON = 1e-06
F32 = jnp.float32
BF16 = jnp.bfloat16
MESH = pl.DeviceIdType.MESH
HIGHEST = lax.Precision.HIGHEST


def unit_target(unit):
    is_query = unit < HEADS // 2
    pair = unit - HEADS // 2
    head = jnp.where(is_query, unit, pair // 2)
    core = head // OWN
    slot = head % OWN + jnp.where(is_query, 0, OWN + OWN * (pair % 2))
    return core, slot


def kernel(
    shape_ref,
    counts_ref,
    patches_ref,
    weight_ref,
    bias_ref,
    block_ref,
    time_ref,
    query_weight_ref,
    pair_weight_ref,
    query_bias_ref,
    pair_bias_ref,
    gain_ref,
    out_ref,
    query_ref,
    pair_ref,
    tokens,
    weight_all,
    bias_own,
    bias_all,
    block_all,
    time_all,
    centred,
    modulated,
    landed,
    columns,
    sending,
    units,
    rows_aug,
    scale_rows,
    cosines,
    sines,
    query_rows,
    key_rows,
    value_rows,
    value_ones,
    query_acc,
    key_acc,
    sums_out,
    sums_in,
    result,
    result_in,
    send_a,
    recv_a,
    send_b,
    recv_b,
    send_c,
    recv_c,
    send_p,
    recv_p,
    send_s,
    recv_s,
    send_o,
    recv_o,
    local,
):
    s = lax.axis_index("seq")
    m = lax.axis_index("mp")
    xz = s // 8
    y = (s // 2) % 4
    core = s % 2
    w = xz * 2 + core
    other = 1 - core
    owner = w < UNITS

    def plane_device(index):
        return (index // 2) * 8 + y * 2 + index % 2

    def remote(src, dst, send, recv, device):
        return pltpu.make_async_remote_copy(
            src_ref=src, dst_ref=dst, send_sem=send, recv_sem=recv, device_id=device, device_id_type=MESH
        )

    units[:, BLOCK:, :] = jnp.zeros((3 * OWN, HD - BLOCK, HD), BF16)

    bias_own[...] = bias_ref[...].reshape(1, HALF)
    query_ref[...] = query_weight_ref[...].reshape(5, 4, HALF)
    pair_ref[...] = pair_weight_ref[...].reshape(5, 4, D)

    barrier = pltpu.get_barrier_semaphore()

    def greet(step, carry):
        pl.semaphore_signal(
            barrier, inc=1, device_id=(plane_device((w + step) % PLANE), m), device_id_type=MESH
        )
        return carry

    lax.fori_loop(1, PLANE, greet, 0)
    for step in range(1, ROWS):
        pl.semaphore_signal(
            barrier,
            inc=1,
            device_id=(xz * 8 + ((y + step) % ROWS) * 2 + core, m),
            device_id_type=MESH,
        )
    pl.semaphore_signal(barrier, inc=1, device_id=(s, 1 - m), device_id_type=MESH)
    pl.semaphore_signal(barrier, inc=1, device_id=(xz * 8 + y * 2 + other, 1 - m), device_id_type=MESH)
    pl.semaphore_wait(barrier, PLANE - 1 + ROWS - 1 + 2)

    sibling = (xz * 8 + y * 2 + other, m)
    partner = (s, 1 - m)
    param_copies = [
        remote(patches_ref, tokens.at[core], send_p.at[0], recv_p.at[0], sibling),
        remote(weight_ref, weight_all.at[m], send_p.at[1], recv_p.at[1], partner),
        remote(bias_own, bias_all.at[m], send_p.at[2], recv_p.at[2], partner),
        remote(block_ref, block_all.at[m], send_p.at[3], recv_p.at[3], partner),
        remote(time_ref.at[:, y], time_all.at[m], send_p.at[4], recv_p.at[4], partner),
    ]
    own_copies = [
        pltpu.make_async_copy(patches_ref, tokens.at[core], local.at[0]),
        pltpu.make_async_copy(weight_ref, weight_all.at[m], local.at[1]),
        pltpu.make_async_copy(bias_own, bias_all.at[m], local.at[2]),
        pltpu.make_async_copy(block_ref, block_all.at[m], local.at[3]),
        pltpu.make_async_copy(time_ref.at[:, y], time_all.at[m], local.at[4]),
    ]
    for copy in param_copies + own_copies:
        copy.start()

    def query_source(unit):
        return query_ref.at[:, :, pl.ds(pl.multiple_of(unit * HD, HD), HD)]

    def pair_source(unit):
        return pair_ref.at[:, :, pl.ds(pl.multiple_of((unit - HEADS // 2) * HD, HD), HD)]

    landing = landed.at[xz, y, pl.ds(core * 5, 5)]

    def scatter(step, carry):
        unit = (w + step) % PLANE

        @pl.when(unit < HEADS // 2)
        def _():
            remote(
                query_source(unit), landing, send_a.at[step], recv_a.at[w], (plane_device(unit), m)
            ).start()

        @pl.when(jnp.logical_and(unit >= HEADS // 2, unit < UNITS))
        def _():
            remote(
                pair_source(unit), landing, send_a.at[step], recv_a.at[w], (plane_device(unit), m)
            ).start()

        return carry

    lax.fori_loop(1, PLANE, scatter, 0)

    @pl.when(w < HEADS // 2)
    def _():
        pltpu.make_async_copy(query_source(w), landing, recv_a.at[w]).start()

    @pl.when(jnp.logical_and(w >= HEADS // 2, owner))
    def _():
        pltpu.make_async_copy(pair_source(w), landing, recv_a.at[w]).start()

    clip = s // 2
    height = shape_ref[1, clip].astype(F32)
    width = shape_ref[2, clip].astype(F32)
    lane = lax.broadcasted_iota(jnp.int32, (1, HD), 1)
    other_pairs = HD // 6
    frame_pairs = HD // 2 - 2 * other_pairs
    pair_id = lane // 2
    in_frame = pair_id < frame_pairs
    in_row = jnp.logical_and(pair_id >= frame_pairs, pair_id < frame_pairs + other_pairs)
    within = jnp.where(
        in_frame,
        pair_id,
        jnp.where(in_row, pair_id - frame_pairs, pair_id - frame_pairs - other_pairs),
    ).astype(F32)
    axis_span = jnp.where(in_frame, 2.0 * frame_pairs, 2.0 * other_pairs).astype(F32)
    inverse = jnp.exp(-(2.0 * within / axis_span) * math.log(10000.0))
    even = lane % 2 == 0
    for part in range(2):
        slot = lax.broadcasted_iota(jnp.int32, (TOK, HD), 0)
        offset = counts_ref[2 * clip] if part else 0
        position = (slot + offset).astype(F32)
        line = jnp.floor((position + 0.5) / width)
        column_pos = position - line * width
        frame_pos = jnp.floor((line + 0.5) / height)
        row_pos = line - frame_pos * height
        angles = jnp.where(in_frame, frame_pos, jnp.where(in_row, row_pos, column_pos)) * inverse
        sine = jnp.sin(angles)
        cosines[part * TOK : (part + 1) * TOK, :] = jnp.cos(angles)
        sines[part * TOK : (part + 1) * TOK, :] = jnp.where(even, -sine, sine)
        valid = slot < counts_ref[2 * clip + part]
        value_ones[part * TOK : (part + 1) * TOK, :] = jnp.where(valid, 1.0, 0.0).astype(BF16)

    for copy in own_copies:
        copy.wait()
    for copy in param_copies:
        copy.wait_recv()
    for part in range(2):
        rows_aug[part * TOK : (part + 1) * TOK, 0:CIN] = tokens[part].T
    rows_aug[:, CIN:] = jnp.where(
        lax.broadcasted_iota(jnp.int32, (2 * TOK, HD - CIN), 1) < 2, 1.0, 0.0
    ).astype(BF16)

    def statistics(step, carry):
        rows = pl.ds(pl.multiple_of(step * 128, 128), 128)
        patch = rows_aug[rows, 0:CIN]
        total = jnp.zeros((128, 1), F32)
        square = jnp.zeros((128, 1), F32)
        for half in range(2):
            embedded = jnp.dot(patch, weight_all[half], preferred_element_type=F32) + bias_all[half]
            total += jnp.sum(embedded, axis=1, keepdims=True)
            square += jnp.sum(embedded * embedded, axis=1, keepdims=True)
        average = total / D
        variance = square / D - average * average
        scale_rows[rows, :] = jnp.broadcast_to(lax.rsqrt(variance + EPSILON), (128, HD))
        return carry

    lax.fori_loop(0, 4, statistics, 0)

    row_mean = (
        jnp.sum(weight_all[0].astype(F32), axis=1, keepdims=True)
        + jnp.sum(weight_all[1].astype(F32), axis=1, keepdims=True)
    ) / D
    bias_mean = (
        jnp.sum(bias_all[0], axis=1, keepdims=True) + jnp.sum(bias_all[1], axis=1, keepdims=True)
    ) / D
    for half in range(2):
        centred[half] = weight_all[half].astype(F32) - row_mean

    def modulate(step, carry):
        rows = pl.multiple_of(step * BLOCK, 16)
        index = lax.broadcasted_iota(jnp.int32, (BLOCK - CIN, HALF), 0)
        for half in range(2):
            scale = 1.0 + time_all[half, step, 1:2, :] + block_all[half, 1:2, :]
            shift = time_all[half, step, 0:1, :] + block_all[half, 0:1, :]
            span = slice(half * HALF, (half + 1) * HALF)
            modulated[pl.ds(rows, CIN), span] = (centred[half] * scale).astype(BF16)
            bias_row = (bias_all[half] - bias_mean) * scale
            bias_low = bias_row - bias_row.astype(BF16).astype(F32)
            shift_low = shift - shift.astype(BF16).astype(F32)
            extra = jnp.where(
                index == 0,
                bias_row,
                jnp.where(
                    index == 1,
                    bias_low,
                    jnp.where(index == 2, shift, jnp.where(index == 3, shift_low, 0.0)),
                ),
            )
            modulated[pl.ds(pl.multiple_of(rows + CIN, 16), BLOCK - CIN), span] = extra.astype(BF16)
        return carry

    lax.fori_loop(0, COLS, modulate, 0)

    @pl.when(owner)
    def _():
        own_landing = pltpu.make_async_copy(landing, landing, recv_a.at[w])
        own_landing.wait()

        def arrive(step, carry):
            source = (w + step) % PLANE
            block = landed.at[source // 2, y, pl.ds((source % 2) * 5, 5)]
            remote(block, block, send_a.at[0], recv_a.at[source], (plane_device(source), m)).wait_recv()
            return carry

        lax.fori_loop(1, PLANE, arrive, 0)
        spread = []
        for step in range(1, ROWS):
            spread.append(
                remote(
                    landed.at[:, y],
                    landed.at[:, y],
                    send_b.at[step - 1],
                    recv_b.at[step - 1],
                    (xz * 8 + ((y + step) % ROWS) * 2 + core, m),
                )
            )
        for copy in spread:
            copy.start()
        for step in range(1, ROWS):
            source = (y + ROWS - step) % ROWS
            remote(
                landed.at[:, source],
                landed.at[:, source],
                send_b.at[step - 1],
                recv_b.at[step - 1],
                (xz * 8 + source * 2 + core, m),
            ).wait_recv()
        columns[...] = landed[...].reshape(D, HD)
        unit_core, unit_slot = unit_target(w)

        for chunk in range(4):
            folded = jnp.dot(
                modulated[chunk * 4 * BLOCK : (chunk + 1) * 4 * BLOCK, :],
                columns[...],
                preferred_element_type=F32,
            )
            for piece in range(4):
                target = chunk * 4 + piece
                block = folded[piece * BLOCK : (piece + 1) * BLOCK]
                extra = block[CIN:]
                bias_row = extra[0:1] + extra[1:2]
                shift_row = extra[2:3] + extra[3:4]
                index = lax.broadcasted_iota(jnp.int32, (BLOCK - CIN, HD), 0)
                tail = jnp.where(
                    index == 0,
                    bias_row,
                    jnp.where(
                        index == 1,
                        bias_row - bias_row.astype(BF16).astype(F32),
                        jnp.where(
                            index == 2,
                            shift_row,
                            jnp.where(
                                index == 3, shift_row - shift_row.astype(BF16).astype(F32), 0.0
                            ),
                        ),
                    ),
                )
                sending[target, 0:CIN, :] = block[:CIN].astype(BF16)
                sending[target, CIN:, :] = tail.astype(BF16)
                device = target * 8 + y * 2 + unit_core

                @pl.when(device != s)
                def _():
                    remote(
                        sending.at[target],
                        units.at[unit_slot, pl.ds(0, BLOCK)],
                        send_c.at[target],
                        recv_c.at[unit_slot],
                        (device, m),
                    ).start()

                @pl.when(device == s)
                def _():
                    pltpu.make_async_copy(
                        sending.at[target], units.at[unit_slot, pl.ds(0, BLOCK)], recv_c.at[unit_slot]
                    ).start()

    def collect(slot, carry):
        block = units.at[slot, pl.ds(0, BLOCK)]
        pltpu.make_async_copy(block, block, recv_c.at[slot]).wait()
        return carry

    query_acc[...] = jnp.zeros_like(query_acc)
    key_acc[...] = jnp.zeros_like(key_acc)

    def raw_rows(slot, rows, bias_row):
        unit = units[slot]
        shift_row = unit[CIN + 2 : CIN + 3].astype(F32) + unit[CIN + 3 : CIN + 4].astype(F32)
        product = jnp.dot(rows_aug[rows, :], unit, preferred_element_type=F32)
        return product * scale_rows[rows, :] + (shift_row + bias_row)

    def rotated(values, rows):
        partner_rows = jnp.where(even, pltpu.roll(values, HD - 1, 1), pltpu.roll(values, 1, 1))
        return values * cosines[rows, :] + partner_rows * sines[rows, :]

    lax.fori_loop(0, 2 * OWN, collect, 0)

    def project(head, carry):
        column = pl.multiple_of((core * OWN + head) * HD, HD)
        query_bias = query_bias_ref[pl.ds(column, HD)].reshape(1, HD)
        key_bias = pair_bias_ref[pl.ds(pl.multiple_of(column * 2, HD), HD)].reshape(1, HD)
        for part in range(2):
            rows = slice(part * TOK, (part + 1) * TOK)
            raw = raw_rows(head, rows, query_bias)
            query_acc[rows, :] += raw * raw
            query_rows[head, rows, :] = rotated(raw * gain_ref[0:1, pl.ds(column, HD)], rows)
            raw = raw_rows(OWN + head, rows, key_bias)
            key_acc[rows, :] += raw * raw
            key_rows[head, rows, :] = rotated(raw * gain_ref[1:2, pl.ds(column, HD)], rows)
        return carry

    lax.fori_loop(0, OWN, project, 0)

    ones = jnp.ones((8, HD), F32)
    contract_lanes = (((1,), (1,)), ((), ()))
    contract_rows = (((0,), (0,)), ((), ()))
    query_sums = lax.dot_general(
        ones, query_acc[...], contract_lanes, precision=HIGHEST, preferred_element_type=F32
    )
    key_sums = lax.dot_general(
        ones, key_acc[...], contract_lanes, precision=HIGHEST, preferred_element_type=F32
    )
    sum_index = lax.broadcasted_iota(jnp.int32, (8, 2 * TOK), 0)
    sums_out[...] = jnp.where(sum_index == 0, query_sums, key_sums)
    sum_copies = [
        remote(sums_out, sums_in.at[0], send_s.at[0], recv_s.at[0], sibling),
        remote(sums_out, sums_in.at[1], send_s.at[1], recv_s.at[1], partner),
        remote(
            sums_out,
            sums_in.at[2],
            send_s.at[2],
            recv_s.at[2],
            (xz * 8 + y * 2 + other, 1 - m),
        ),
    ]
    for copy in sum_copies:
        copy.start()

    def collect_value(head, carry):
        return collect(2 * OWN + head, carry)

    lax.fori_loop(0, OWN, collect_value, 0)

    def values(head, carry):
        column = pl.multiple_of(((core * OWN + head) * 2 + 1) * HD, HD)
        value_bias = pair_bias_ref[pl.ds(column, HD)].reshape(1, HD)
        for part in range(2):
            rows = slice(part * TOK, (part + 1) * TOK)
            raw = raw_rows(2 * OWN + head, rows, value_bias)
            slot = lax.broadcasted_iota(jnp.int32, (TOK, HD), 0)
            kept = jnp.where(slot < counts_ref[2 * clip + part], raw, 0.0)
            value_rows[head, rows, :] = kept.astype(BF16)
        return carry

    lax.fori_loop(0, OWN, values, 0)

    for copy in sum_copies:
        copy.wait_recv()
    square_sums = sums_out[...] + sums_in[0] + sums_in[1] + sums_in[2]
    factors = lax.rsqrt(square_sums / (HEADS * HD) + EPSILON)
    query_factor = lax.dot_general(
        jnp.where(sum_index == 0, factors * (HD**-0.5 * math.log2(math.e)), 0.0),
        ones,
        contract_rows,
        precision=HIGHEST,
        preferred_element_type=F32,
    )
    key_factor = lax.dot_general(
        jnp.where(sum_index == 1, factors, 0.0),
        ones,
        contract_rows,
        precision=HIGHEST,
        preferred_element_type=F32,
    )
    query_acc[...] = query_factor
    key_acc[...] = jnp.where(value_ones[...].astype(F32) > 0.0, key_factor, 0.0)

    def attend(head, carry):
        keys = (key_rows[head] * key_acc[...]).astype(BF16)
        for part in range(2):
            rows = slice(part * TOK, (part + 1) * TOK)
            queries = (query_rows[head, rows, :] * query_acc[rows, :]).astype(BF16)
            scores = lax.dot_general(queries, keys, contract_lanes, preferred_element_type=F32)
            weights = jnp.exp2(scores).astype(BF16)
            numerator = jnp.dot(weights, value_rows[head], preferred_element_type=F32)
            totals = jnp.dot(weights, value_ones[...], preferred_element_type=F32)
            slot = lax.broadcasted_iota(jnp.int32, (TOK, HD), 0)
            kept = jnp.where(slot < counts_ref[2 * clip + part], numerator / totals, 0.0)
            result[part, head] = kept.astype(BF16)
        remote(
            result.at[other, head], result_in.at[head], send_o.at[head], recv_o.at[head], sibling
        ).start()
        return carry

    lax.fori_loop(0, OWN, attend, 0)

    for side in range(2):
        @pl.when(core == side)
        def _():
            for head in range(OWN):
                column = (side * OWN + head) * HD
                out_ref[:, column : column + HD] = result[side, head]

    for head in range(OWN):
        remote(
            result.at[other, head], result_in.at[head], send_o.at[head], recv_o.at[head], sibling
        ).wait()

    for side in range(2):
        @pl.when(core == side)
        def _():
            for head in range(OWN):
                column = ((1 - side) * OWN + head) * HD
                out_ref[:, column : column + HD] = result_in[head]

    for copy in param_copies + sum_copies:
        copy.wait_send()

    def sent(step, carry):
        @pl.when((w + step) % PLANE < UNITS)
        def _():
            remote(query_source(0), landing, send_a.at[step], recv_a.at[w], partner).wait_send()

        return carry

    lax.fori_loop(1, PLANE, sent, 0)

    @pl.when(owner)
    def _():
        for step in range(1, ROWS):
            remote(
                landed.at[:, y], landed.at[:, y], send_b.at[step - 1], recv_b.at[step - 1], partner
            ).wait_send()
        unit_core, unit_slot = unit_target(w)

        def sent_block(target, carry):
            @pl.when(target * 8 + y * 2 + unit_core != s)
            def _():
                remote(
                    sending.at[target],
                    units.at[unit_slot, pl.ds(0, BLOCK)],
                    send_c.at[target],
                    recv_c.at[unit_slot],
                    partner,
                ).wait_send()

            return carry

        lax.fori_loop(0, COLS, sent_block, 0)


def shards(
    patches,
    clip_shape,
    shard_counts,
    patch_weight,
    patch_bias,
    time_mod,
    block_mod,
    w_query,
    query_bias,
    w_keyvalue,
    keyvalue_bias,
    norm_gain,
):
    vmem = pl.BlockSpec(memory_space=pltpu.VMEM)
    smem = pl.BlockSpec(memory_space=pltpu.SMEM)
    anywhere = pl.BlockSpec(memory_space=pl.ANY)
    dma = pltpu.SemaphoreType.DMA
    return pl.pallas_call(
        kernel,
        out_shape=jax.ShapeDtypeStruct((TOK, HALF), BF16),
        in_specs=[smem, smem, vmem, vmem, vmem, vmem, anywhere, vmem, vmem, vmem, vmem, vmem],
        out_specs=vmem,
        scratch_shapes=[
            pltpu.VMEM((5, 4, HALF), BF16),
            pltpu.VMEM((5, 4, D), BF16),
            pltpu.VMEM((2, CIN, TOK), BF16),
            pltpu.VMEM((2, CIN, HALF), BF16),
            pltpu.VMEM((1, HALF), F32),
            pltpu.VMEM((2, 1, HALF), F32),
            pltpu.VMEM((2, 2, HALF), F32),
            pltpu.VMEM((2, COLS, 2, HALF), F32),
            pltpu.VMEM((2, CIN, HALF), F32),
            pltpu.VMEM((COLS * BLOCK, D), BF16),
            pltpu.VMEM((COLS, ROWS, 10, 4, HD), BF16),
            pltpu.VMEM((D, HD), BF16),
            pltpu.VMEM((COLS, BLOCK, HD), BF16),
            pltpu.VMEM((3 * OWN, HD, HD), BF16),
            pltpu.VMEM((2 * TOK, HD), BF16),
            pltpu.VMEM((2 * TOK, HD), F32),
            pltpu.VMEM((2 * TOK, HD), F32),
            pltpu.VMEM((2 * TOK, HD), F32),
            pltpu.VMEM((OWN, 2 * TOK, HD), F32),
            pltpu.VMEM((OWN, 2 * TOK, HD), F32),
            pltpu.VMEM((OWN, 2 * TOK, HD), BF16),
            pltpu.VMEM((2 * TOK, HD), BF16),
            pltpu.VMEM((2 * TOK, HD), F32),
            pltpu.VMEM((2 * TOK, HD), F32),
            pltpu.VMEM((8, 2 * TOK), F32),
            pltpu.VMEM((3, 8, 2 * TOK), F32),
            pltpu.VMEM((2, OWN, TOK, HD), BF16),
            pltpu.VMEM((OWN, TOK, HD), BF16),
            dma((PLANE,)),
            dma((PLANE,)),
            dma((ROWS - 1,)),
            dma((ROWS - 1,)),
            dma((COLS,)),
            dma((3 * OWN,)),
            dma((5,)),
            dma((5,)),
            dma((3,)),
            dma((3,)),
            dma((OWN,)),
            dma((OWN,)),
            dma((5,)),
        ],
        compiler_params=pltpu.CompilerParams(
            collective_id=0, has_side_effects=True, vmem_limit_bytes=60 << 20
        ),
    )(
        clip_shape.T,
        shard_counts,
        patches.T,
        patch_weight,
        patch_bias,
        block_mod,
        time_mod.reshape(COLS, ROWS, 2, HALF),
        w_query,
        w_keyvalue,
        query_bias,
        keyvalue_bias,
        norm_gain,
    )


def solution(mesh):
    return jax.shard_map(
        shards,
        mesh=mesh,
        in_specs=(
            P("seq", None),
            P(),
            P(),
            P(None, "mp"),
            P("mp"),
            P(None, None, "mp"),
            P(None, "mp"),
            P("seq", "mp"),
            P("mp"),
            P("seq", "mp"),
            P("mp"),
            P(None, "mp"),
        ),
        out_specs=P("seq", "mp"),
        check_vma=False,
    )
```

time: 570 us -> 60.9 us (0.11)
  the two profiles are of different devices: /device:TPU:1 before, /device:TPU:39 now
where the time goes in v1:
time: 60.9 us; the launch traced here: 60.8 us
  Pallas kernels  58.8 us (97%)
  local copies, waits for them, and re-layouts  1.97 us (3%)
    pallas_call x1, Pallas kernels, shards(): pl.pallas_call(kernel, out_shape=jax.ShapeDtypeStruct((TOK, HALF), BF16),...  58.8 us
    unnamed x1, local copies, waits for them, and re-layouts  1.97 us

profile of v1, /device:TPU:39, one launch (start us, length us, event | category | flops | bytes accessed | tf_op | source)
XLA Modules:
  0.0 60.8 jit_solution(940231386420166453)
XLA Ops:
  0.0 58.8 %shard_map.118 = bf16[256,1280]{1,0:T(8,128)(2,1)} custom-call(s32[3,64]{1,0:T(4,128)} %bitcast.5, s32[128]{0:T(128)} %counts_ref.1, bf16[64,256]{1,0:T(8,128)(2,1)} %bitcast.4, bf16[64,1280]{1,0:T(8,128)(2,1)} %weight_ref.1, f32[1280]{0:T(1024)} %bias_ref.1, f32[2,1280]{1,0:T(2,128)} %block_ref.1, f32[16,4,2,1280]{3,2,1,0:T(2,128)} %bitcast.3, ...), custom_call_target="tpu_custom_call" | custom-call | tf_op jit(solution)/shard_map/pallas_call | solution.py:562
  58.8 2.0 %copy.14 = bf16[256,1280]{1,0:T(8,128)(2,1)} copy(bf16[256,1280]{1,0:T(8,128)(2,1)} %shard_map.118) | data formatting | bytes 1310720

commit v2 on v1

--- a/solution.py
+++ b/solution.py
@@ -15,8 +15,7 @@
 CIN = 64
 TOK = 256
 PLANE = 32
-COLS = 16
-ROWS = 4
+CLIPS_HERE = 16
 UNITS = 30
 OWN = 5
 BLOCK = 80
@@ -94,15 +93,21 @@
 ):
     s = lax.axis_index("seq")
     m = lax.axis_index("mp")
-    xz = s // 8
-    y = (s // 2) % 4
+    x_lo = s // (2 * PLANE)
+    chip = (s // 2) % PLANE
     core = s % 2
-    w = xz * 2 + core
     other = 1 - core
-    owner = w < UNITS
-
-    def plane_device(index):
-        return (index // 2) * 8 + y * 2 + index % 2
+    owner = chip < UNITS
+    unit_core, unit_slot = unit_target(chip)
+    crossing = jnp.logical_and(owner, unit_core != core)
+
+    def plane_device(index, side):
+        return (x_lo * 2 * PLANE + index * 2 + side, m)
+
+    sibling = plane_device(chip, other)
+    partner = (s, 1 - m)
+    diagonal = (sibling[0], 1 - m)
+    neighbour = (s + 2 * PLANE * (1 - 2 * x_lo), m)
 
     def remote(src, dst, send, recv, device):
         return pltpu.make_async_remote_copy(
@@ -119,37 +124,45 @@
 
     def greet(step, carry):
         pl.semaphore_signal(
-            barrier, inc=1, device_id=(plane_device((w + step) % PLANE), m), device_id_type=MESH
+            barrier, inc=1, device_id=plane_device((chip + step) % PLANE, core), device_id_type=MESH
         )
         return carry
 
     lax.fori_loop(1, PLANE, greet, 0)
-    for step in range(1, ROWS):
-        pl.semaphore_signal(
-            barrier,
-            inc=1,
-            device_id=(xz * 8 + ((y + step) % ROWS) * 2 + core, m),
-            device_id_type=MESH,
-        )
-    pl.semaphore_signal(barrier, inc=1, device_id=(s, 1 - m), device_id_type=MESH)
-    pl.semaphore_signal(barrier, inc=1, device_id=(xz * 8 + y * 2 + other, 1 - m), device_id_type=MESH)
-    pl.semaphore_wait(barrier, PLANE - 1 + ROWS - 1 + 2)
-
-    sibling = (xz * 8 + y * 2 + other, m)
-    partner = (s, 1 - m)
+    for device in (sibling, partner, diagonal, neighbour):
+        pl.semaphore_signal(barrier, inc=1, device_id=device, device_id_type=MESH)
+
+    @pl.when(chip // CLIPS_HERE != core)
+    def _():
+        def greet_owner(step, carry):
+            unit = jnp.where(
+                step < OWN, core * OWN + step, HEADS // 2 + core * 2 * OWN + step - OWN
+            )
+            pl.semaphore_signal(
+                barrier, inc=1, device_id=plane_device(unit, other), device_id_type=MESH
+            )
+            return carry
+
+        lax.fori_loop(0, 3 * OWN, greet_owner, 0)
+
+    pl.semaphore_wait(barrier, PLANE - 1 + 4 + jnp.where(crossing, CLIPS_HERE, 0))
+
+    half_rows = pl.ds(pl.multiple_of(core * (CIN // 2), CIN // 2), CIN // 2)
+    own_clips = pl.ds(x_lo * PLANE + core * CLIPS_HERE, CLIPS_HERE)
     param_copies = [
         remote(patches_ref, tokens.at[core], send_p.at[0], recv_p.at[0], sibling),
-        remote(weight_ref, weight_all.at[m], send_p.at[1], recv_p.at[1], partner),
+        remote(weight_ref.at[half_rows], weight_all.at[m, core], send_p.at[1], recv_p.at[1], partner),
         remote(bias_own, bias_all.at[m], send_p.at[2], recv_p.at[2], partner),
         remote(block_ref, block_all.at[m], send_p.at[3], recv_p.at[3], partner),
-        remote(time_ref.at[:, y], time_all.at[m], send_p.at[4], recv_p.at[4], partner),
+        remote(time_ref.at[own_clips], time_all.at[m], send_p.at[4], recv_p.at[4], partner),
     ]
     own_copies = [
         pltpu.make_async_copy(patches_ref, tokens.at[core], local.at[0]),
-        pltpu.make_async_copy(weight_ref, weight_all.at[m], local.at[1]),
+        pltpu.make_async_copy(weight_ref.at[pl.ds(0, CIN // 2)], weight_all.at[m, 0], local.at[1]),
+        pltpu.make_async_copy(weight_ref.at[pl.ds(CIN // 2, CIN // 2)], weight_all.at[m, 1], local.at[5]),
         pltpu.make_async_copy(bias_own, bias_all.at[m], local.at[2]),
         pltpu.make_async_copy(block_ref, block_all.at[m], local.at[3]),
-        pltpu.make_async_copy(time_ref.at[:, y], time_all.at[m], local.at[4]),
+        pltpu.make_async_copy(time_ref.at[own_clips], time_all.at[m], local.at[4]),
     ]
     for copy in param_copies + own_copies:
         copy.start()
@@ -160,34 +173,34 @@
     def pair_source(unit):
         return pair_ref.at[:, :, pl.ds(pl.multiple_of((unit - HEADS // 2) * HD, HD), HD)]
 
-    landing = landed.at[xz, y, pl.ds(core * 5, 5)]
+    landing = landed.at[x_lo, chip, core]
 
     def scatter(step, carry):
-        unit = (w + step) % PLANE
+        unit = (chip + step) % PLANE
 
         @pl.when(unit < HEADS // 2)
         def _():
             remote(
-                query_source(unit), landing, send_a.at[step], recv_a.at[w], (plane_device(unit), m)
+                query_source(unit), landing, send_a.at[step], recv_a.at[chip], plane_device(unit, core)
             ).start()
 
         @pl.when(jnp.logical_and(unit >= HEADS // 2, unit < UNITS))
         def _():
             remote(
-                pair_source(unit), landing, send_a.at[step], recv_a.at[w], (plane_device(unit), m)
+                pair_source(unit), landing, send_a.at[step], recv_a.at[chip], plane_device(unit, core)
             ).start()
 
         return carry
 
     lax.fori_loop(1, PLANE, scatter, 0)
 
-    @pl.when(w < HEADS // 2)
+    @pl.when(chip < HEADS // 2)
     def _():
-        pltpu.make_async_copy(query_source(w), landing, recv_a.at[w]).start()
-
-    @pl.when(jnp.logical_and(w >= HEADS // 2, owner))
+        pltpu.make_async_copy(query_source(chip), landing, recv_a.at[chip]).start()
+
+    @pl.when(jnp.logical_and(chip >= HEADS // 2, owner))
     def _():
-        pltpu.make_async_copy(pair_source(w), landing, recv_a.at[w]).start()
+        pltpu.make_async_copy(pair_source(chip), landing, recv_a.at[chip]).start()
 
     clip = s // 2
     height = shape_ref[1, clip].astype(F32)
@@ -221,9 +234,35 @@
         valid = slot < counts_ref[2 * clip + part]
         value_ones[part * TOK : (part + 1) * TOK, :] = jnp.where(valid, 1.0, 0.0).astype(BF16)
 
+    here = landed.at[x_lo, :, core]
+    there = landed.at[1 - x_lo, :, core]
+    to_sibling = remote(here, here, send_b.at[0], recv_b.at[0], sibling)
+    to_neighbour = remote(here, here, send_b.at[1], recv_b.at[1], neighbour)
+    passed_on = remote(there, there, send_b.at[2], recv_b.at[2], sibling)
+
+    @pl.when(owner)
+    def _():
+        pltpu.make_async_copy(landing, landing, recv_a.at[chip]).wait()
+
+        def arrive(step, carry):
+            source = (chip + step) % PLANE
+            block = landed.at[x_lo, source, core]
+            remote(
+                block, block, send_a.at[0], recv_a.at[source], plane_device(source, core)
+            ).wait_recv()
+            return carry
+
+        lax.fori_loop(1, PLANE, arrive, 0)
+        to_neighbour.start()
+        to_sibling.start()
+
+    param_copies[1].wait_recv()
+    weight_block = weight_all.at[1 - m, core]
+    shared = remote(weight_block, weight_block, send_p.at[5], recv_p.at[5], sibling)
+    shared.start()
     for copy in own_copies:
         copy.wait()
-    for copy in param_copies:
+    for copy in param_copies[:1] + param_copies[2:] + [shared]:
         copy.wait_recv()
     for part in range(2):
         rows_aug[part * TOK : (part + 1) * TOK, 0:CIN] = tokens[part].T
@@ -237,7 +276,7 @@
         total = jnp.zeros((128, 1), F32)
         square = jnp.zeros((128, 1), F32)
         for half in range(2):
-            embedded = jnp.dot(patch, weight_all[half], preferred_element_type=F32) + bias_all[half]
+            embedded = jnp.dot(patch, weight_all[half].reshape(CIN, HALF), preferred_element_type=F32) + bias_all[half]
             total += jnp.sum(embedded, axis=1, keepdims=True)
             square += jnp.sum(embedded * embedded, axis=1, keepdims=True)
         average = total / D
@@ -248,14 +287,14 @@
     lax.fori_loop(0, 4, statistics, 0)
 
     row_mean = (
-        jnp.sum(weight_all[0].astype(F32), axis=1, keepdims=True)
-        + jnp.sum(weight_all[1].astype(F32), axis=1, keepdims=True)
+        jnp.sum(weight_all[0].reshape(CIN, HALF).astype(F32), axis=1, keepdims=True)
+        + jnp.sum(weight_all[1].reshape(CIN, HALF).astype(F32), axis=1, keepdims=True)
     ) / D
     bias_mean = (
         jnp.sum(bias_all[0], axis=1, keepdims=True) + jnp.sum(bias_all[1], axis=1, keepdims=True)
     ) / D
     for half in range(2):
-        centred[half] = weight_all[half].astype(F32) - row_mean
+        centred[half] = weight_all[half].reshape(CIN, HALF).astype(F32) - row_mean
 
     def modulate(step, carry):
         rows = pl.multiple_of(step * BLOCK, 16)
@@ -280,48 +319,20 @@
             modulated[pl.ds(pl.multiple_of(rows + CIN, 16), BLOCK - CIN), span] = extra.astype(BF16)
         return carry
 
-    lax.fori_loop(0, COLS, modulate, 0)
+    lax.fori_loop(0, CLIPS_HERE, modulate, 0)
 
     @pl.when(owner)
     def _():
-        own_landing = pltpu.make_async_copy(landing, landing, recv_a.at[w])
-        own_landing.wait()
-
-        def arrive(step, carry):
-            source = (w + step) % PLANE
-            block = landed.at[source // 2, y, pl.ds((source % 2) * 5, 5)]
-            remote(block, block, send_a.at[0], recv_a.at[source], (plane_device(source), m)).wait_recv()
-            return carry
-
-        lax.fori_loop(1, PLANE, arrive, 0)
-        spread = []
-        for step in range(1, ROWS):
-            spread.append(
-                remote(
-                    landed.at[:, y],
-                    landed.at[:, y],
-                    send_b.at[step - 1],
-                    recv_b.at[step - 1],
-                    (xz * 8 + ((y + step) % ROWS) * 2 + core, m),
-                )
-            )
-        for copy in spread:
-            copy.start()
-        for step in range(1, ROWS):
-            source = (y + ROWS - step) % ROWS
-            remote(
-                landed.at[:, source],
-                landed.at[:, source],
-                send_b.at[step - 1],
-                recv_b.at[step - 1],
-                (xz * 8 + source * 2 + core, m),
-            ).wait_recv()
+        to_neighbour.wait_recv()
+        passed_on.start()
+        to_sibling.wait_recv()
+        passed_on.wait_recv()
         columns[...] = landed[...].reshape(D, HD)
-        unit_core, unit_slot = unit_target(w)
-
-        for chunk in range(4):
+
+        for turn in range(4):
+            chunk = (turn + chip) % 4
             folded = jnp.dot(
-                modulated[chunk * 4 * BLOCK : (chunk + 1) * 4 * BLOCK, :],
+                modulated[pl.ds(pl.multiple_of(chunk * 4 * BLOCK, 4 * BLOCK), 4 * BLOCK), :],
                 columns[...],
                 preferred_element_type=F32,
             )
@@ -349,19 +360,22 @@
                 )
                 sending[target, 0:CIN, :] = block[:CIN].astype(BF16)
                 sending[target, CIN:, :] = tail.astype(BF16)
-                device = target * 8 + y * 2 + unit_core
-
-                @pl.when(device != s)
+
+            for piece in range(4):
+                target = chunk * 4 + (piece + chip // 4) % 4
+                device = plane_device(core * CLIPS_HERE + target, unit_core)
+
+                @pl.when(device[0] != s)
                 def _():
                     remote(
                         sending.at[target],
                         units.at[unit_slot, pl.ds(0, BLOCK)],
                         send_c.at[target],
                         recv_c.at[unit_slot],
-                        (device, m),
+                        device,
                     ).start()
 
-                @pl.when(device == s)
+                @pl.when(device[0] == s)
                 def _():
                     pltpu.make_async_copy(
                         sending.at[target], units.at[unit_slot, pl.ds(0, BLOCK)], recv_c.at[unit_slot]
@@ -422,7 +436,7 @@
             sums_in.at[2],
             send_s.at[2],
             recv_s.at[2],
-            (xz * 8 + y * 2 + other, 1 - m),
+            diagonal,
         ),
     ]
     for copy in sum_copies:
@@ -505,13 +519,13 @@
                 column = ((1 - side) * OWN + head) * HD
                 out_ref[:, column : column + HD] = result_in[head]
 
-    for copy in param_copies + sum_copies:
+    for copy in param_copies + [shared] + sum_copies:
         copy.wait_send()
 
     def sent(step, carry):
-        @pl.when((w + step) % PLANE < UNITS)
+        @pl.when((chip + step) % PLANE < UNITS)
         def _():
-            remote(query_source(0), landing, send_a.at[step], recv_a.at[w], partner).wait_send()
+            remote(query_source(0), landing, send_a.at[step], recv_a.at[chip], partner).wait_send()
 
         return carry
 
@@ -519,14 +533,11 @@
 
     @pl.when(owner)
     def _():
-        for step in range(1, ROWS):
-            remote(
-                landed.at[:, y], landed.at[:, y], send_b.at[step - 1], recv_b.at[step - 1], partner
-            ).wait_send()
-        unit_core, unit_slot = unit_target(w)
+        for copy in (to_sibling, to_neighbour, passed_on):
+            copy.wait_send()
 
         def sent_block(target, carry):
-            @pl.when(target * 8 + y * 2 + unit_core != s)
+            @pl.when(plane_device(core * CLIPS_HERE + target, unit_core)[0] != s)
             def _():
                 remote(
                     sending.at[target],
@@ -538,7 +549,7 @@
 
             return carry
 
-        lax.fori_loop(0, COLS, sent_block, 0)
+        lax.fori_loop(0, CLIPS_HERE, sent_block, 0)
 
 
 def shards(
@@ -568,16 +579,16 @@
             pltpu.VMEM((5, 4, HALF), BF16),
             pltpu.VMEM((5, 4, D), BF16),
             pltpu.VMEM((2, CIN, TOK), BF16),
-            pltpu.VMEM((2, CIN, HALF), BF16),
+            pltpu.VMEM((2, 2, CIN // 2, HALF), BF16),
             pltpu.VMEM((1, HALF), F32),
             pltpu.VMEM((2, 1, HALF), F32),
             pltpu.VMEM((2, 2, HALF), F32),
-            pltpu.VMEM((2, COLS, 2, HALF), F32),
+            pltpu.VMEM((2, CLIPS_HERE, 2, HALF), F32),
             pltpu.VMEM((2, CIN, HALF), F32),
-            pltpu.VMEM((COLS * BLOCK, D), BF16),
-            pltpu.VMEM((COLS, ROWS, 10, 4, HD), BF16),
+            pltpu.VMEM((CLIPS_HERE * BLOCK, D), BF16),
+            pltpu.VMEM((2, PLANE, 2, 5, 4, HD), BF16),
             pltpu.VMEM((D, HD), BF16),
-            pltpu.VMEM((COLS, BLOCK, HD), BF16),
+            pltpu.VMEM((CLIPS_HERE, BLOCK, HD), BF16),
             pltpu.VMEM((3 * OWN, HD, HD), BF16),
             pltpu.VMEM((2 * TOK, HD), BF16),
             pltpu.VMEM((2 * TOK, HD), F32),
@@ -595,17 +606,17 @@
             pltpu.VMEM((OWN, TOK, HD), BF16),
             dma((PLANE,)),
             dma((PLANE,)),
-            dma((ROWS - 1,)),
-            dma((ROWS - 1,)),
-            dma((COLS,)),
+            dma((3,)),
+            dma((3,)),
+            dma((CLIPS_HERE,)),
             dma((3 * OWN,)),
-            dma((5,)),
-            dma((5,)),
+            dma((6,)),
+            dma((6,)),
             dma((3,)),
             dma((3,)),
             dma((OWN,)),
             dma((OWN,)),
-            dma((5,)),
+            dma((6,)),
         ],
         compiler_params=pltpu.CompilerParams(
             collective_id=0, has_side_effects=True, vmem_limit_bytes=60 << 20
@@ -617,7 +628,7 @@
         patch_weight,
         patch_bias,
         block_mod,
-        time_mod.reshape(COLS, ROWS, 2, HALF),
+        time_mod,
         w_query,
         w_keyvalue,
         query_bias,

time: 60.9 us -> 56.5 us (0.928)
  the two profiles are of different devices: /device:TPU:39 before, /device:TPU:1 now
where the time goes in v2:
time: 56.5 us; the launch traced here: 56.3 us
  Pallas kernels  54.4 us (96%)
  local copies, waits for them, and re-layouts  1.97 us (3%)
    pallas_call x1, Pallas kernels, shards(): pl.pallas_call(kernel, out_shape=jax.ShapeDtypeStruct((TOK, HALF), BF16),...  54.4 us
    unnamed x1, local copies, waits for them, and re-layouts  1.97 us

profile of v2, /device:TPU:1, one launch (start us, length us, event | category | flops | bytes accessed | tf_op | source)
XLA Modules:
  0.0 56.3 jit_solution(158186909795125115)
XLA Ops:
  0.0 54.4 %shard_map.118 = bf16[256,1280]{1,0:T(8,128)(2,1)} custom-call(s32[3,64]{1,0:T(4,128)} %bitcast.3, s32[128]{0:T(128)} %counts_ref.1, bf16[64,256]{1,0:T(8,128)(2,1)} %bitcast.2, bf16[64,1280]{1,0:T(8,128)(2,1)} %weight_ref.1, f32[1280]{0:T(1024)} %bias_ref.1, f32[2,1280]{1,0:T(2,128)} %block_ref.1, f32[64,2,1280]{2,1,0:T(2,128)} %time_ref.1, ...), custom_call_target="tpu_custom_call" | custom-call | tf_op jit(solution)/shard_map/pallas_call | solution.py:573
  54.4 2.0 %copy.14 = bf16[256,1280]{1,0:T(8,128)(2,1)} copy(bf16[256,1280]{1,0:T(8,128)(2,1)} %shard_map.118) | data formatting | bytes 1310720

commit v3 on v2

--- a/solution.py
+++ b/solution.py
@@ -45,15 +45,19 @@
     time_ref,
     query_weight_ref,
     pair_weight_ref,
+    query_bias_hbm,
+    pair_bias_hbm,
+    gain_hbm,
+    out_ref,
+    query_weight,
+    pair_weight,
     query_bias_ref,
     pair_bias_ref,
     gain_ref,
-    out_ref,
     query_ref,
     pair_ref,
     tokens,
     weight_all,
-    bias_own,
     bias_all,
     block_all,
     time_all,
@@ -70,13 +74,12 @@
     query_rows,
     key_rows,
     value_rows,
-    value_ones,
+    valid_rows,
     query_acc,
     key_acc,
     sums_out,
     sums_in,
     result,
-    result_in,
     send_a,
     recv_a,
     send_b,
@@ -90,6 +93,7 @@
     send_o,
     recv_o,
     local,
+    local_o,
 ):
     s = lax.axis_index("seq")
     m = lax.axis_index("mp")
@@ -114,12 +118,6 @@
             src_ref=src, dst_ref=dst, send_sem=send, recv_sem=recv, device_id=device, device_id_type=MESH
         )
 
-    units[:, BLOCK:, :] = jnp.zeros((3 * OWN, HD - BLOCK, HD), BF16)
-
-    bias_own[...] = bias_ref[...].reshape(1, HALF)
-    query_ref[...] = query_weight_ref[...].reshape(5, 4, HALF)
-    pair_ref[...] = pair_weight_ref[...].reshape(5, 4, D)
-
     barrier = pltpu.get_barrier_semaphore()
 
     def greet(step, carry):
@@ -145,62 +143,37 @@
 
         lax.fori_loop(0, 3 * OWN, greet_owner, 0)
 
-    pl.semaphore_wait(barrier, PLANE - 1 + 4 + jnp.where(crossing, CLIPS_HERE, 0))
-
     half_rows = pl.ds(pl.multiple_of(core * (CIN // 2), CIN // 2), CIN // 2)
     own_clips = pl.ds(x_lo * PLANE + core * CLIPS_HERE, CLIPS_HERE)
-    param_copies = [
-        remote(patches_ref, tokens.at[core], send_p.at[0], recv_p.at[0], sibling),
-        remote(weight_ref.at[half_rows], weight_all.at[m, core], send_p.at[1], recv_p.at[1], partner),
-        remote(bias_own, bias_all.at[m], send_p.at[2], recv_p.at[2], partner),
-        remote(block_ref, block_all.at[m], send_p.at[3], recv_p.at[3], partner),
-        remote(time_ref.at[own_clips], time_all.at[m], send_p.at[4], recv_p.at[4], partner),
+
+    weight_copies = [
+        pltpu.make_async_copy(query_weight_ref, query_weight, local.at[0]),
+        pltpu.make_async_copy(pair_weight_ref, pair_weight, local.at[1]),
     ]
     own_copies = [
-        pltpu.make_async_copy(patches_ref, tokens.at[core], local.at[0]),
-        pltpu.make_async_copy(weight_ref.at[pl.ds(0, CIN // 2)], weight_all.at[m, 0], local.at[1]),
-        pltpu.make_async_copy(weight_ref.at[pl.ds(CIN // 2, CIN // 2)], weight_all.at[m, 1], local.at[5]),
-        pltpu.make_async_copy(bias_own, bias_all.at[m], local.at[2]),
-        pltpu.make_async_copy(block_ref, block_all.at[m], local.at[3]),
-        pltpu.make_async_copy(time_ref.at[own_clips], time_all.at[m], local.at[4]),
+        pltpu.make_async_copy(patches_ref, tokens.at[core], local.at[2]),
+        pltpu.make_async_copy(weight_ref.at[pl.ds(0, CIN // 2)], weight_all.at[m, 0], local.at[3]),
+        pltpu.make_async_copy(
+            weight_ref.at[pl.ds(CIN // 2, CIN // 2)], weight_all.at[m, 1], local.at[4]
+        ),
+        pltpu.make_async_copy(bias_ref, bias_all.at[m, 0], local.at[5]),
+        pltpu.make_async_copy(block_ref, block_all.at[m], local.at[6]),
+        pltpu.make_async_copy(time_ref.at[own_clips], time_all.at[m], local.at[7]),
+        pltpu.make_async_copy(query_bias_hbm, query_bias_ref.at[0], local.at[8]),
+        pltpu.make_async_copy(pair_bias_hbm, pair_bias_ref.at[0], local.at[9]),
+        pltpu.make_async_copy(gain_hbm, gain_ref, local.at[10]),
     ]
-    for copy in param_copies + own_copies:
+    for copy in weight_copies + own_copies:
         copy.start()
 
-    def query_source(unit):
-        return query_ref.at[:, :, pl.ds(pl.multiple_of(unit * HD, HD), HD)]
-
-    def pair_source(unit):
-        return pair_ref.at[:, :, pl.ds(pl.multiple_of((unit - HEADS // 2) * HD, HD), HD)]
-
-    landing = landed.at[x_lo, chip, core]
-
-    def scatter(step, carry):
-        unit = (chip + step) % PLANE
-
-        @pl.when(unit < HEADS // 2)
-        def _():
-            remote(
-                query_source(unit), landing, send_a.at[step], recv_a.at[chip], plane_device(unit, core)
-            ).start()
-
-        @pl.when(jnp.logical_and(unit >= HEADS // 2, unit < UNITS))
-        def _():
-            remote(
-                pair_source(unit), landing, send_a.at[step], recv_a.at[chip], plane_device(unit, core)
-            ).start()
-
-        return carry
-
-    lax.fori_loop(1, PLANE, scatter, 0)
-
-    @pl.when(chip < HEADS // 2)
-    def _():
-        pltpu.make_async_copy(query_source(chip), landing, recv_a.at[chip]).start()
-
-    @pl.when(jnp.logical_and(chip >= HEADS // 2, owner))
-    def _():
-        pltpu.make_async_copy(pair_source(chip), landing, recv_a.at[chip]).start()
+    units[:, BLOCK:, :] = jnp.zeros((3 * OWN, HD - BLOCK, HD), BF16)
+    rows_aug[:, CIN:] = jnp.where(
+        lax.broadcasted_iota(jnp.int32, (2 * TOK, HD - CIN), 1) < 2, 1.0, 0.0
+    ).astype(BF16)
+    for copy in weight_copies:
+        copy.wait()
+    query_ref[...] = query_weight[...].reshape(5, 4, HALF)
+    pair_ref[...] = pair_weight[...].reshape(5, 4, D)
 
     clip = s // 2
     height = shape_ref[1, clip].astype(F32)
@@ -232,7 +205,57 @@
         cosines[part * TOK : (part + 1) * TOK, :] = jnp.cos(angles)
         sines[part * TOK : (part + 1) * TOK, :] = jnp.where(even, -sine, sine)
         valid = slot < counts_ref[2 * clip + part]
-        value_ones[part * TOK : (part + 1) * TOK, :] = jnp.where(valid, 1.0, 0.0).astype(BF16)
+        kept = jnp.where(valid, 1.0, 0.0).astype(BF16)
+        valid_rows[part * TOK : (part + 1) * TOK, :] = jnp.where(valid, 1.0, 0.0)
+        for head in range(OWN):
+            value_rows[head, part * TOK : (part + 1) * TOK, HD:] = kept
+
+    pl.semaphore_wait(barrier, PLANE - 1 + 4 + jnp.where(crossing, CLIPS_HERE, 0))
+
+    param_copies = [
+        remote(patches_ref, tokens.at[core], send_p.at[0], recv_p.at[0], sibling),
+        remote(weight_ref.at[half_rows], weight_all.at[m, core], send_p.at[1], recv_p.at[1], partner),
+        remote(bias_ref, bias_all.at[m, 0], send_p.at[2], recv_p.at[2], partner),
+        remote(block_ref, block_all.at[m], send_p.at[3], recv_p.at[3], partner),
+        remote(time_ref.at[own_clips], time_all.at[m], send_p.at[4], recv_p.at[4], partner),
+    ]
+    for copy in param_copies:
+        copy.start()
+
+    def query_source(unit):
+        return query_ref.at[:, :, pl.ds(pl.multiple_of(unit * HD, HD), HD)]
+
+    def pair_source(unit):
+        return pair_ref.at[:, :, pl.ds(pl.multiple_of((unit - HEADS // 2) * HD, HD), HD)]
+
+    landing = landed.at[x_lo, chip, core]
+
+    def scatter(step, carry):
+        unit = (chip + step) % PLANE
+
+        @pl.when(unit < HEADS // 2)
+        def _():
+            remote(
+                query_source(unit), landing, send_a.at[step], recv_a.at[chip], plane_device(unit, core)
+            ).start()
+
+        @pl.when(jnp.logical_and(unit >= HEADS // 2, unit < UNITS))
+        def _():
+            remote(
+                pair_source(unit), landing, send_a.at[step], recv_a.at[chip], plane_device(unit, core)
+            ).start()
+
+        return carry
+
+    lax.fori_loop(1, PLANE, scatter, 0)
+
+    @pl.when(chip < HEADS // 2)
+    def _():
+        pltpu.make_async_copy(query_source(chip), landing, recv_a.at[chip]).start()
+
+    @pl.when(jnp.logical_and(chip >= HEADS // 2, owner))
+    def _():
+        pltpu.make_async_copy(pair_source(chip), landing, recv_a.at[chip]).start()
 
     here = landed.at[x_lo, :, core]
     there = landed.at[1 - x_lo, :, core]
@@ -266,9 +289,6 @@
         copy.wait_recv()
     for part in range(2):
         rows_aug[part * TOK : (part + 1) * TOK, 0:CIN] = tokens[part].T
-    rows_aug[:, CIN:] = jnp.where(
-        lax.broadcasted_iota(jnp.int32, (2 * TOK, HD - CIN), 1) < 2, 1.0, 0.0
-    ).astype(BF16)
 
     def statistics(step, carry):
         rows = pl.ds(pl.multiple_of(step * 128, 128), 128)
@@ -389,11 +409,10 @@
     query_acc[...] = jnp.zeros_like(query_acc)
     key_acc[...] = jnp.zeros_like(key_acc)
 
-    def raw_rows(slot, rows, bias_row):
+    def unit_rows(slot):
         unit = units[slot]
         shift_row = unit[CIN + 2 : CIN + 3].astype(F32) + unit[CIN + 3 : CIN + 4].astype(F32)
-        product = jnp.dot(rows_aug[rows, :], unit, preferred_element_type=F32)
-        return product * scale_rows[rows, :] + (shift_row + bias_row)
+        return unit, shift_row
 
     def rotated(values, rows):
         partner_rows = jnp.where(even, pltpu.roll(values, HD - 1, 1), pltpu.roll(values, 1, 1))
@@ -403,16 +422,21 @@
 
     def project(head, carry):
         column = pl.multiple_of((core * OWN + head) * HD, HD)
-        query_bias = query_bias_ref[pl.ds(column, HD)].reshape(1, HD)
-        key_bias = pair_bias_ref[pl.ds(pl.multiple_of(column * 2, HD), HD)].reshape(1, HD)
+        query_unit, query_shift = unit_rows(head)
+        key_unit, key_shift = unit_rows(OWN + head)
+        both = jnp.concatenate([query_unit, key_unit], axis=1)
+        query_shift += query_bias_ref[0:1, pl.ds(column, HD)]
+        key_shift += pair_bias_ref[0:1, pl.ds(pl.multiple_of(column * 2, HD), HD)]
         for part in range(2):
             rows = slice(part * TOK, (part + 1) * TOK)
-            raw = raw_rows(head, rows, query_bias)
+            product = jnp.dot(rows_aug[rows, :], both, preferred_element_type=F32)
+            scale = scale_rows[rows, :]
+            raw = product[:, :HD] * scale + query_shift
             query_acc[rows, :] += raw * raw
-            query_rows[head, rows, :] = rotated(raw * gain_ref[0:1, pl.ds(column, HD)], rows)
-            raw = raw_rows(OWN + head, rows, key_bias)
+            query_rows[head, rows, :] = raw
+            raw = product[:, HD:] * scale + key_shift
             key_acc[rows, :] += raw * raw
-            key_rows[head, rows, :] = rotated(raw * gain_ref[1:2, pl.ds(column, HD)], rows)
+            key_rows[head, rows, :] = raw
         return carry
 
     lax.fori_loop(0, OWN, project, 0)
@@ -442,6 +466,18 @@
     for copy in sum_copies:
         copy.start()
 
+    def rotate(head, carry):
+        column = pl.multiple_of((core * OWN + head) * HD, HD)
+        query_gain = gain_ref[0:1, pl.ds(column, HD)]
+        key_gain = gain_ref[1:2, pl.ds(column, HD)]
+        for part in range(2):
+            rows = slice(part * TOK, (part + 1) * TOK)
+            query_rows[head, rows, :] = rotated(query_rows[head, rows, :] * query_gain, rows)
+            key_rows[head, rows, :] = rotated(key_rows[head, rows, :] * key_gain, rows)
+        return carry
+
+    lax.fori_loop(0, OWN, rotate, 0)
+
     def collect_value(head, carry):
         return collect(2 * OWN + head, carry)
 
@@ -449,13 +485,13 @@
 
     def values(head, carry):
         column = pl.multiple_of(((core * OWN + head) * 2 + 1) * HD, HD)
-        value_bias = pair_bias_ref[pl.ds(column, HD)].reshape(1, HD)
+        unit, shift = unit_rows(2 * OWN + head)
+        shift += pair_bias_ref[0:1, pl.ds(column, HD)]
         for part in range(2):
             rows = slice(part * TOK, (part + 1) * TOK)
-            raw = raw_rows(2 * OWN + head, rows, value_bias)
-            slot = lax.broadcasted_iota(jnp.int32, (TOK, HD), 0)
-            kept = jnp.where(slot < counts_ref[2 * clip + part], raw, 0.0)
-            value_rows[head, rows, :] = kept.astype(BF16)
+            product = jnp.dot(rows_aug[rows, :], unit, preferred_element_type=F32)
+            raw = product * scale_rows[rows, :] + shift
+            value_rows[head, rows, :HD] = jnp.where(valid_rows[rows, :] > 0.0, raw, 0.0).astype(BF16)
         return carry
 
     lax.fori_loop(0, OWN, values, 0)
@@ -479,7 +515,17 @@
         preferred_element_type=F32,
     )
     query_acc[...] = query_factor
-    key_acc[...] = jnp.where(value_ones[...].astype(F32) > 0.0, key_factor, 0.0)
+    key_acc[...] = jnp.where(valid_rows[...] > 0.0, key_factor, 0.0)
+
+    def own_result(head):
+        span = pl.ds(pl.multiple_of((core * OWN + head) * HD, HD), HD)
+        return pltpu.make_async_copy(result.at[core, head], out_ref.at[:, span], local_o.at[head])
+
+    def other_result(head):
+        span = pl.ds(pl.multiple_of((core * OWN + head) * HD, HD), HD)
+        return remote(
+            result.at[other, head], out_ref.at[:, span], send_o.at[head], recv_o.at[head], sibling
+        )
 
     def attend(head, carry):
         keys = (key_rows[head] * key_acc[...]).astype(BF16)
@@ -488,36 +534,21 @@
             queries = (query_rows[head, rows, :] * query_acc[rows, :]).astype(BF16)
             scores = lax.dot_general(queries, keys, contract_lanes, preferred_element_type=F32)
             weights = jnp.exp2(scores).astype(BF16)
-            numerator = jnp.dot(weights, value_rows[head], preferred_element_type=F32)
-            totals = jnp.dot(weights, value_ones[...], preferred_element_type=F32)
-            slot = lax.broadcasted_iota(jnp.int32, (TOK, HD), 0)
-            kept = jnp.where(slot < counts_ref[2 * clip + part], numerator / totals, 0.0)
+            summed = jnp.dot(weights, value_rows[head], preferred_element_type=F32)
+            kept = jnp.where(valid_rows[rows, :] > 0.0, summed[:, :HD] / summed[:, HD:], 0.0)
             result[part, head] = kept.astype(BF16)
-        remote(
-            result.at[other, head], result_in.at[head], send_o.at[head], recv_o.at[head], sibling
-        ).start()
+        other_result(head).start()
+        own_result(head).start()
         return carry
 
     lax.fori_loop(0, OWN, attend, 0)
 
-    for side in range(2):
-        @pl.when(core == side)
-        def _():
-            for head in range(OWN):
-                column = (side * OWN + head) * HD
-                out_ref[:, column : column + HD] = result[side, head]
-
     for head in range(OWN):
-        remote(
-            result.at[other, head], result_in.at[head], send_o.at[head], recv_o.at[head], sibling
-        ).wait()
-
-    for side in range(2):
-        @pl.when(core == side)
-        def _():
-            for head in range(OWN):
-                column = ((1 - side) * OWN + head) * HD
-                out_ref[:, column : column + HD] = result_in[head]
+        span = pl.ds(pl.multiple_of((other * OWN + head) * HD, HD), HD)
+        arrived = out_ref.at[:, span]
+        remote(arrived, arrived, send_o.at[head], recv_o.at[head], sibling).wait_recv()
+        other_result(head).wait_send()
+        own_result(head).wait()
 
     for copy in param_copies + [shared] + sum_copies:
         copy.wait_send()
@@ -566,21 +597,24 @@
     keyvalue_bias,
     norm_gain,
 ):
-    vmem = pl.BlockSpec(memory_space=pltpu.VMEM)
     smem = pl.BlockSpec(memory_space=pltpu.SMEM)
     anywhere = pl.BlockSpec(memory_space=pl.ANY)
     dma = pltpu.SemaphoreType.DMA
     return pl.pallas_call(
         kernel,
         out_shape=jax.ShapeDtypeStruct((TOK, HALF), BF16),
-        in_specs=[smem, smem, vmem, vmem, vmem, vmem, anywhere, vmem, vmem, vmem, vmem, vmem],
-        out_specs=vmem,
+        in_specs=[smem, smem] + [anywhere] * 10,
+        out_specs=anywhere,
         scratch_shapes=[
+            pltpu.VMEM((20, HALF), BF16),
+            pltpu.VMEM((20, D), BF16),
+            pltpu.VMEM((1, HALF), F32),
+            pltpu.VMEM((1, D), F32),
+            pltpu.VMEM((2, HALF), F32),
             pltpu.VMEM((5, 4, HALF), BF16),
             pltpu.VMEM((5, 4, D), BF16),
             pltpu.VMEM((2, CIN, TOK), BF16),
             pltpu.VMEM((2, 2, CIN // 2, HALF), BF16),
-            pltpu.VMEM((1, HALF), F32),
             pltpu.VMEM((2, 1, HALF), F32),
             pltpu.VMEM((2, 2, HALF), F32),
             pltpu.VMEM((2, CLIPS_HERE, 2, HALF), F32),
@@ -596,14 +630,13 @@
             pltpu.VMEM((2 * TOK, HD), F32),
             pltpu.VMEM((OWN, 2 * TOK, HD), F32),
             pltpu.VMEM((OWN, 2 * TOK, HD), F32),
-            pltpu.VMEM((OWN, 2 * TOK, HD), BF16),
-            pltpu.VMEM((2 * TOK, HD), BF16),
+            pltpu.VMEM((OWN, 2 * TOK, 2 * HD), BF16),
+            pltpu.VMEM((2 * TOK, HD), F32),
             pltpu.VMEM((2 * TOK, HD), F32),
             pltpu.VMEM((2 * TOK, HD), F32),
             pltpu.VMEM((8, 2 * TOK), F32),
             pltpu.VMEM((3, 8, 2 * TOK), F32),
             pltpu.VMEM((2, OWN, TOK, HD), BF16),
-            pltpu.VMEM((OWN, TOK, HD), BF16),
             dma((PLANE,)),
             dma((PLANE,)),
             dma((3,)),
@@ -616,7 +649,8 @@
             dma((3,)),
             dma((OWN,)),
             dma((OWN,)),
-            dma((6,)),
+            dma((11,)),
+            dma((OWN,)),
         ],
         compiler_params=pltpu.CompilerParams(
             collective_id=0, has_side_effects=True, vmem_limit_bytes=60 << 20

time: 56.5 us -> 52.8 us (0.935)
  Pallas kernels: 54.4 us -> 50.7 us
    pallas_call x1, Pallas kernels: 54.4 us -> 50.7 us  [shards(): pl.pallas_call(kernel, out_shape=jax.ShapeDtypeStruct((TOK, HALF), BF16),...]
where the time goes in v3:
time: 52.8 us; the launch traced here: 52.7 us
  Pallas kernels  50.7 us (96%)
  local copies, waits for them, and re-layouts  1.97 us (4%)
    pallas_call x1, Pallas kernels, shards(): pl.pallas_call(kernel, out_shape=jax.ShapeDtypeStruct((TOK, HALF), BF16),...  50.7 us
    unnamed x1, local copies, waits for them, and re-layouts  1.97 us

profile of v3, /device:TPU:1, one launch (start us, length us, event | category | flops | bytes accessed | tf_op | source)
XLA Modules:
  0.0 52.7 jit_solution(10152259295401863528)
XLA Ops:
  0.0 50.7 %shard_map.118 = bf16[256,1280]{1,0:T(8,128)(2,1)} custom-call(s32[3,64]{1,0:T(4,128)} %bitcast.3, s32[128]{0:T(128)} %counts_ref.1, bf16[64,256]{1,0:T(8,128)(2,1)} %bitcast.2, bf16[64,1280]{1,0:T(8,128)(2,1)} %weight_ref.1, f32[1280]{0:T(1024)} %bias_ref.1, f32[2,1280]{1,0:T(2,128)} %block_ref.1, f32[64,2,1280]{2,1,0:T(2,128)} %time_ref.1, ...), custom_call_target="tpu_custom_call" | custom-call | tf_op jit(solution)/shard_map/pallas_call | solution.py:603
  50.7 2.0 %copy.14 = bf16[256,1280]{1,0:T(8,128)(2,1)} copy(bf16[256,1280]{1,0:T(8,128)(2,1)} %shard_map.118) | data formatting | bytes 1310720

commit v4 on v3

--- a/solution.py
+++ b/solution.py
@@ -18,12 +18,13 @@
 CLIPS_HERE = 16
 UNITS = 30
 OWN = 5
+GROUPS = 8
 BLOCK = 80
+WIRE = 72
 EPSILON = 1e-06
 F32 = jnp.float32
 BF16 = jnp.bfloat16
 MESH = pl.DeviceIdType.MESH
-HIGHEST = lax.Precision.HIGHEST
 
 
 def unit_target(unit):
@@ -54,13 +55,14 @@
     query_bias_ref,
     pair_bias_ref,
     gain_ref,
-    query_ref,
-    pair_ref,
+    rows_ref,
     tokens,
     weight_all,
     bias_all,
     block_all,
     time_all,
+    row_sums,
+    row_sums_in,
     centred,
     modulated,
     landed,
@@ -112,6 +114,7 @@
     partner = (s, 1 - m)
     diagonal = (sibling[0], 1 - m)
     neighbour = (s + 2 * PLANE * (1 - 2 * x_lo), m)
+    adjacent = (neighbour[0], 1 - m)
 
     def remote(src, dst, send, recv, device):
         return pltpu.make_async_remote_copy(
@@ -120,14 +123,18 @@
 
     barrier = pltpu.get_barrier_semaphore()
 
-    def greet(step, carry):
+    def far_first(index):
+        return PLANE // 2 + (1 - 2 * (index % 2)) * ((index + 1) // 2)
+
+    def greet(index, carry):
+        step = far_first(index)
         pl.semaphore_signal(
             barrier, inc=1, device_id=plane_device((chip + step) % PLANE, core), device_id_type=MESH
         )
         return carry
 
-    lax.fori_loop(1, PLANE, greet, 0)
-    for device in (sibling, partner, diagonal, neighbour):
+    lax.fori_loop(0, PLANE - 1, greet, 0)
+    for device in (neighbour, adjacent, partner, diagonal, sibling):
         pl.semaphore_signal(barrier, inc=1, device_id=device, device_id_type=MESH)
 
     @pl.when(chip // CLIPS_HERE != core)
@@ -145,6 +152,7 @@
 
     half_rows = pl.ds(pl.multiple_of(core * (CIN // 2), CIN // 2), CIN // 2)
     own_clips = pl.ds(x_lo * PLANE + core * CLIPS_HERE, CLIPS_HERE)
+    adjacent_clips = pl.ds((1 - x_lo) * PLANE + core * CLIPS_HERE, CLIPS_HERE)
 
     weight_copies = [
         pltpu.make_async_copy(query_weight_ref, query_weight, local.at[0]),
@@ -166,14 +174,14 @@
     for copy in weight_copies + own_copies:
         copy.start()
 
-    units[:, BLOCK:, :] = jnp.zeros((3 * OWN, HD - BLOCK, HD), BF16)
+    units[:, WIRE:, :] = jnp.zeros((3 * OWN, HD - WIRE, HD), BF16)
     rows_aug[:, CIN:] = jnp.where(
         lax.broadcasted_iota(jnp.int32, (2 * TOK, HD - CIN), 1) < 2, 1.0, 0.0
     ).astype(BF16)
     for copy in weight_copies:
         copy.wait()
-    query_ref[...] = query_weight[...].reshape(5, 4, HALF)
-    pair_ref[...] = pair_weight[...].reshape(5, 4, D)
+    rows_ref[:, :, :HALF] = query_weight[...].reshape(5, 4, HALF)
+    rows_ref[:, :, HALF:] = pair_weight[...].reshape(5, 4, D)
 
     clip = s // 2
     height = shape_ref[1, clip].astype(F32)
@@ -210,126 +218,100 @@
         for head in range(OWN):
             value_rows[head, part * TOK : (part + 1) * TOK, HD:] = kept
 
-    pl.semaphore_wait(barrier, PLANE - 1 + 4 + jnp.where(crossing, CLIPS_HERE, 0))
+    for copy in own_copies:
+        copy.wait()
+    for part in range(2):
+        block_rows = slice(part * CIN // 2, (part + 1) * CIN // 2)
+        row_sums[block_rows, :] = jnp.broadcast_to(
+            jnp.sum(weight_all[m, part].astype(F32), axis=1, keepdims=True), (CIN // 2, HD)
+        )
+    row_sums[CIN:, :] = jnp.broadcast_to(jnp.sum(bias_all[m], axis=1, keepdims=True), (8, HD))
+
+    pl.semaphore_wait(barrier, PLANE - 1 + 5 + jnp.where(crossing, CLIPS_HERE, 0))
 
     param_copies = [
         remote(patches_ref, tokens.at[core], send_p.at[0], recv_p.at[0], sibling),
-        remote(weight_ref.at[half_rows], weight_all.at[m, core], send_p.at[1], recv_p.at[1], partner),
-        remote(bias_ref, bias_all.at[m, 0], send_p.at[2], recv_p.at[2], partner),
-        remote(block_ref, block_all.at[m], send_p.at[3], recv_p.at[3], partner),
-        remote(time_ref.at[own_clips], time_all.at[m], send_p.at[4], recv_p.at[4], partner),
+        remote(weight_ref.at[half_rows], weight_all.at[m, core], send_p.at[1], recv_p.at[1], adjacent),
+        remote(bias_ref, bias_all.at[m, 0], send_p.at[2], recv_p.at[2], adjacent),
+        remote(block_ref, block_all.at[m], send_p.at[3], recv_p.at[3], adjacent),
+        remote(time_ref.at[adjacent_clips], time_all.at[m], send_p.at[4], recv_p.at[4], adjacent),
     ]
+    def source_of(unit):
+        return rows_ref.at[:, :, pl.ds(pl.multiple_of(unit * HD, HD), HD)]
+
+    landing = landed.at[x_lo, chip, core]
+
+    def scatter(index, carry):
+        step = far_first(index)
+        unit = (chip + step) % PLANE
+
+        @pl.when(unit < UNITS)
+        def _():
+            remote(
+                source_of(unit), landing, send_a.at[step], recv_a.at[chip], plane_device(unit, core)
+            ).start()
+
+        return carry
+
+    lax.fori_loop(0, PLANE - 1, scatter, 0)
+
+    @pl.when(owner)
+    def _():
+        pltpu.make_async_copy(source_of(chip), landing, recv_a.at[chip]).start()
+
+    sums_copy = remote(row_sums, row_sums_in, send_p.at[6], recv_p.at[6], adjacent)
+    sums_copy.start()
     for copy in param_copies:
         copy.start()
 
-    def query_source(unit):
-        return query_ref.at[:, :, pl.ds(pl.multiple_of(unit * HD, HD), HD)]
-
-    def pair_source(unit):
-        return pair_ref.at[:, :, pl.ds(pl.multiple_of((unit - HEADS // 2) * HD, HD), HD)]
-
-    landing = landed.at[x_lo, chip, core]
-
-    def scatter(step, carry):
-        unit = (chip + step) % PLANE
-
-        @pl.when(unit < HEADS // 2)
+    depth = chip // 4
+
+    def group_of(index):
+        return pl.ds((depth + (0, 1, 7, 2, 6, 3, 5, 4)[index]) % GROUPS * 4, 4)
+
+    def to_sibling(index):
+        block = landed.at[x_lo, group_of(index), core]
+        return remote(block, block, send_b.at[index], recv_b.at[index], sibling)
+
+    def to_neighbour(index):
+        block = landed.at[x_lo, group_of(index), core]
+        slot = GROUPS + index
+        return remote(block, block, send_b.at[slot], recv_b.at[slot], neighbour)
+
+    def passed_on(index):
+        block = landed.at[1 - x_lo, group_of(index), core]
+        slot = 2 * GROUPS + index
+        return remote(block, block, send_b.at[slot], recv_b.at[slot], sibling)
+
+    def hand_on(groups):
+        @pl.when(owner)
         def _():
-            remote(
-                query_source(unit), landing, send_a.at[step], recv_a.at[chip], plane_device(unit, core)
-            ).start()
-
-        @pl.when(jnp.logical_and(unit >= HEADS // 2, unit < UNITS))
-        def _():
-            remote(
-                pair_source(unit), landing, send_a.at[step], recv_a.at[chip], plane_device(unit, core)
-            ).start()
-
-        return carry
-
-    lax.fori_loop(1, PLANE, scatter, 0)
-
-    @pl.when(chip < HEADS // 2)
-    def _():
-        pltpu.make_async_copy(query_source(chip), landing, recv_a.at[chip]).start()
-
-    @pl.when(jnp.logical_and(chip >= HEADS // 2, owner))
-    def _():
-        pltpu.make_async_copy(pair_source(chip), landing, recv_a.at[chip]).start()
-
-    here = landed.at[x_lo, :, core]
-    there = landed.at[1 - x_lo, :, core]
-    to_sibling = remote(here, here, send_b.at[0], recv_b.at[0], sibling)
-    to_neighbour = remote(here, here, send_b.at[1], recv_b.at[1], neighbour)
-    passed_on = remote(there, there, send_b.at[2], recv_b.at[2], sibling)
-
-    @pl.when(owner)
-    def _():
-        pltpu.make_async_copy(landing, landing, recv_a.at[chip]).wait()
-
-        def arrive(step, carry):
-            source = (chip + step) % PLANE
-            block = landed.at[x_lo, source, core]
-            remote(
-                block, block, send_a.at[0], recv_a.at[source], plane_device(source, core)
-            ).wait_recv()
-            return carry
-
-        lax.fori_loop(1, PLANE, arrive, 0)
-        to_neighbour.start()
-        to_sibling.start()
-
-    param_copies[1].wait_recv()
-    weight_block = weight_all.at[1 - m, core]
-    shared = remote(weight_block, weight_block, send_p.at[5], recv_p.at[5], sibling)
-    shared.start()
-    for copy in own_copies:
-        copy.wait()
-    for copy in param_copies[:1] + param_copies[2:] + [shared]:
-        copy.wait_recv()
-    for part in range(2):
-        rows_aug[part * TOK : (part + 1) * TOK, 0:CIN] = tokens[part].T
-
-    def statistics(step, carry):
-        rows = pl.ds(pl.multiple_of(step * 128, 128), 128)
-        patch = rows_aug[rows, 0:CIN]
-        total = jnp.zeros((128, 1), F32)
-        square = jnp.zeros((128, 1), F32)
-        for half in range(2):
-            embedded = jnp.dot(patch, weight_all[half].reshape(CIN, HALF), preferred_element_type=F32) + bias_all[half]
-            total += jnp.sum(embedded, axis=1, keepdims=True)
-            square += jnp.sum(embedded * embedded, axis=1, keepdims=True)
-        average = total / D
-        variance = square / D - average * average
-        scale_rows[rows, :] = jnp.broadcast_to(lax.rsqrt(variance + EPSILON), (128, HD))
-        return carry
-
-    lax.fori_loop(0, 4, statistics, 0)
-
-    row_mean = (
-        jnp.sum(weight_all[0].reshape(CIN, HALF).astype(F32), axis=1, keepdims=True)
-        + jnp.sum(weight_all[1].reshape(CIN, HALF).astype(F32), axis=1, keepdims=True)
-    ) / D
-    bias_mean = (
-        jnp.sum(bias_all[0], axis=1, keepdims=True) + jnp.sum(bias_all[1], axis=1, keepdims=True)
-    ) / D
-    for half in range(2):
-        centred[half] = weight_all[half].reshape(CIN, HALF).astype(F32) - row_mean
-
-    def modulate(step, carry):
-        rows = pl.multiple_of(step * BLOCK, 16)
-        index = lax.broadcasted_iota(jnp.int32, (BLOCK - CIN, HALF), 0)
-        for half in range(2):
+            for index in groups:
+                first = (depth + (0, 1, 7, 2, 6, 3, 5, 4)[index]) % GROUPS * 4
+                for step in range(4):
+                    block = landed.at[x_lo, first + step, core]
+                    pltpu.make_async_copy(block, block, recv_a.at[first + step]).wait()
+                to_neighbour(index).start()
+                to_sibling(index).start()
+
+    def modulate_half(half):
+        mean = (row_sums[:, 0:1] + row_sums_in[:, 0:1]) / D
+        centred[...] = weight_all[half].reshape(CIN, HALF).astype(F32) - mean[:CIN]
+        bias_row = bias_all[half] - mean[CIN : CIN + 1]
+        span = pl.ds(pl.multiple_of(half * HALF, HALF), HALF)
+
+        def modulate(step, carry):
+            rows = pl.multiple_of(step * BLOCK, 16)
+            index = lax.broadcasted_iota(jnp.int32, (BLOCK - CIN, HALF), 0)
             scale = 1.0 + time_all[half, step, 1:2, :] + block_all[half, 1:2, :]
             shift = time_all[half, step, 0:1, :] + block_all[half, 0:1, :]
-            span = slice(half * HALF, (half + 1) * HALF)
-            modulated[pl.ds(rows, CIN), span] = (centred[half] * scale).astype(BF16)
-            bias_row = (bias_all[half] - bias_mean) * scale
-            bias_low = bias_row - bias_row.astype(BF16).astype(F32)
+            modulated[pl.ds(rows, CIN), span] = (centred[...] * scale).astype(BF16)
+            bias_scaled = bias_row * scale
+            bias_low = bias_scaled - bias_scaled.astype(BF16).astype(F32)
             shift_low = shift - shift.astype(BF16).astype(F32)
             extra = jnp.where(
                 index == 0,
-                bias_row,
+                bias_scaled,
                 jnp.where(
                     index == 1,
                     bias_low,
@@ -337,20 +319,41 @@
                 ),
             )
             modulated[pl.ds(pl.multiple_of(rows + CIN, 16), BLOCK - CIN), span] = extra.astype(BF16)
-        return carry
-
-    lax.fori_loop(0, CLIPS_HERE, modulate, 0)
+            return carry
+
+        lax.fori_loop(0, CLIPS_HERE, modulate, 0)
+
+    hand_on(range(0, 3))
+    sums_copy.wait_recv()
+    modulate_half(m)
+    hand_on(range(3, GROUPS))
+
+    param_copies[1].wait_recv()
+    weight_block = weight_all.at[1 - m, core]
+    shared = remote(weight_block, weight_block, send_p.at[5], recv_p.at[5], sibling)
+    shared.start()
 
     @pl.when(owner)
     def _():
-        to_neighbour.wait_recv()
-        passed_on.start()
-        to_sibling.wait_recv()
-        passed_on.wait_recv()
+        for index in range(GROUPS):
+            to_neighbour(index).wait_recv()
+            passed_on(index).start()
+
+    for copy in param_copies[:1] + param_copies[2:] + [shared]:
+        copy.wait_recv()
+    modulate_half(1 - m)
+
+    @pl.when(owner)
+    def _():
+        for index in range(GROUPS):
+            to_sibling(index).wait_recv()
+            passed_on(index).wait_recv()
         columns[...] = landed[...].reshape(D, HD)
 
+        ahead = (core * 4 - depth) % GROUPS
+        backward = jnp.logical_or(ahead <= 2, ahead == 7)
         for turn in range(4):
-            chunk = (turn + chip) % 4
+            chunk = jnp.where(backward, 3 - turn, turn)
             folded = jnp.dot(
                 modulated[pl.ds(pl.multiple_of(chunk * 4 * BLOCK, 4 * BLOCK), 4 * BLOCK), :],
                 columns[...],
@@ -388,8 +391,8 @@
                 @pl.when(device[0] != s)
                 def _():
                     remote(
-                        sending.at[target],
-                        units.at[unit_slot, pl.ds(0, BLOCK)],
+                        sending.at[target, pl.ds(0, WIRE)],
+                        units.at[unit_slot, pl.ds(0, WIRE)],
                         send_c.at[target],
                         recv_c.at[unit_slot],
                         device,
@@ -398,11 +401,34 @@
                 @pl.when(device[0] == s)
                 def _():
                     pltpu.make_async_copy(
-                        sending.at[target], units.at[unit_slot, pl.ds(0, BLOCK)], recv_c.at[unit_slot]
+                        sending.at[target, pl.ds(0, WIRE)], units.at[unit_slot, pl.ds(0, WIRE)], recv_c.at[unit_slot]
                     ).start()
 
+
+    for part in range(2):
+        rows_aug[part * TOK : (part + 1) * TOK, 0:CIN] = tokens[part].T
+
+    def statistics(step, carry):
+        rows = pl.ds(pl.multiple_of(step * 128, 128), 128)
+        patch = rows_aug[rows, 0:CIN]
+        total = jnp.zeros((128, 1), F32)
+        square = jnp.zeros((128, 1), F32)
+        for half in range(2):
+            embedded = (
+                jnp.dot(patch, weight_all[half].reshape(CIN, HALF), preferred_element_type=F32)
+                + bias_all[half]
+            )
+            total += jnp.sum(embedded, axis=1, keepdims=True)
+            square += jnp.sum(embedded * embedded, axis=1, keepdims=True)
+        average = total / D
+        variance = square / D - average * average
+        scale_rows[rows, :] = jnp.broadcast_to(lax.rsqrt(variance + EPSILON), (128, HD))
+        return carry
+
+    lax.fori_loop(0, 4, statistics, 0)
+
     def collect(slot, carry):
-        block = units.at[slot, pl.ds(0, BLOCK)]
+        block = units.at[slot, pl.ds(0, WIRE)]
         pltpu.make_async_copy(block, block, recv_c.at[slot]).wait()
         return carry
 
@@ -441,15 +467,28 @@
 
     lax.fori_loop(0, OWN, project, 0)
 
-    ones = jnp.ones((8, HD), F32)
+    ones = jnp.ones((16, 2 * HD), BF16)
     contract_lanes = (((1,), (1,)), ((), ()))
     contract_rows = (((0,), (0,)), ((), ()))
-    query_sums = lax.dot_general(
-        ones, query_acc[...], contract_lanes, precision=HIGHEST, preferred_element_type=F32
-    )
-    key_sums = lax.dot_general(
-        ones, key_acc[...], contract_lanes, precision=HIGHEST, preferred_element_type=F32
-    )
+
+    def split_sums(values):
+        high = values.astype(BF16)
+        low = (values - high.astype(F32)).astype(BF16)
+        both = jnp.concatenate([high, low], axis=1)
+        return lax.dot_general(ones, both, contract_lanes, preferred_element_type=F32)[:8]
+
+    def split_columns(row):
+        high = row.astype(BF16).astype(F32)
+        middle = (row - high).astype(BF16).astype(F32)
+        low = row - high - middle
+        index = lax.broadcasted_iota(jnp.int32, (16, 2 * TOK), 0)
+        parts = jnp.where(
+            index == 0, high, jnp.where(index == 1, middle, jnp.where(index == 2, low, 0.0))
+        ).astype(BF16)
+        return lax.dot_general(parts, ones[:, :HD], contract_rows, preferred_element_type=F32)
+
+    query_sums = split_sums(query_acc[...])
+    key_sums = split_sums(key_acc[...])
     sum_index = lax.broadcasted_iota(jnp.int32, (8, 2 * TOK), 0)
     sums_out[...] = jnp.where(sum_index == 0, query_sums, key_sums)
     sum_copies = [
@@ -500,20 +539,8 @@
         copy.wait_recv()
     square_sums = sums_out[...] + sums_in[0] + sums_in[1] + sums_in[2]
     factors = lax.rsqrt(square_sums / (HEADS * HD) + EPSILON)
-    query_factor = lax.dot_general(
-        jnp.where(sum_index == 0, factors * (HD**-0.5 * math.log2(math.e)), 0.0),
-        ones,
-        contract_rows,
-        precision=HIGHEST,
-        preferred_element_type=F32,
-    )
-    key_factor = lax.dot_general(
-        jnp.where(sum_index == 1, factors, 0.0),
-        ones,
-        contract_rows,
-        precision=HIGHEST,
-        preferred_element_type=F32,
-    )
+    query_factor = split_columns(factors[0:1] * (HD**-0.5 * math.log2(math.e)))
+    key_factor = split_columns(factors[1:2])
     query_acc[...] = query_factor
     key_acc[...] = jnp.where(valid_rows[...] > 0.0, key_factor, 0.0)
 
@@ -541,7 +568,7 @@
         own_result(head).start()
         return carry
 
-    lax.fori_loop(0, OWN, attend, 0)
+    lax.fori_loop(0, OWN, attend, 0, unroll=True)
 
     for head in range(OWN):
         span = pl.ds(pl.multiple_of((other * OWN + head) * HD, HD), HD)
@@ -550,13 +577,13 @@
         other_result(head).wait_send()
         own_result(head).wait()
 
-    for copy in param_copies + [shared] + sum_copies:
+    for copy in param_copies + [sums_copy, shared] + sum_copies:
         copy.wait_send()
 
     def sent(step, carry):
         @pl.when((chip + step) % PLANE < UNITS)
         def _():
-            remote(query_source(0), landing, send_a.at[step], recv_a.at[chip], partner).wait_send()
+            remote(source_of(0), landing, send_a.at[step], recv_a.at[chip], partner).wait_send()
 
         return carry
 
@@ -564,15 +591,17 @@
 
     @pl.when(owner)
     def _():
-        for copy in (to_sibling, to_neighbour, passed_on):
-            copy.wait_send()
+        for index in range(GROUPS):
+            to_sibling(index).wait_send()
+            to_neighbour(index).wait_send()
+            passed_on(index).wait_send()
 
         def sent_block(target, carry):
             @pl.when(plane_device(core * CLIPS_HERE + target, unit_core)[0] != s)
             def _():
                 remote(
-                    sending.at[target],
-                    units.at[unit_slot, pl.ds(0, BLOCK)],
+                    sending.at[target, pl.ds(0, WIRE)],
+                    units.at[unit_slot, pl.ds(0, WIRE)],
                     send_c.at[target],
                     recv_c.at[unit_slot],
                     partner,
@@ -611,14 +640,15 @@
             pltpu.VMEM((1, HALF), F32),
             pltpu.VMEM((1, D), F32),
             pltpu.VMEM((2, HALF), F32),
-            pltpu.VMEM((5, 4, HALF), BF16),
-            pltpu.VMEM((5, 4, D), BF16),
+            pltpu.VMEM((5, 4, HALF + D), BF16),
             pltpu.VMEM((2, CIN, TOK), BF16),
             pltpu.VMEM((2, 2, CIN // 2, HALF), BF16),
             pltpu.VMEM((2, 1, HALF), F32),
             pltpu.VMEM((2, 2, HALF), F32),
             pltpu.VMEM((2, CLIPS_HERE, 2, HALF), F32),
-            pltpu.VMEM((2, CIN, HALF), F32),
+            pltpu.VMEM((CIN + 8, HD), F32),
+            pltpu.VMEM((CIN + 8, HD), F32),
+            pltpu.VMEM((CIN, HALF), F32),
             pltpu.VMEM((CLIPS_HERE * BLOCK, D), BF16),
             pltpu.VMEM((2, PLANE, 2, 5, 4, HD), BF16),
             pltpu.VMEM((D, HD), BF16),
@@ -639,12 +669,12 @@
             pltpu.VMEM((2, OWN, TOK, HD), BF16),
             dma((PLANE,)),
             dma((PLANE,)),
-            dma((3,)),
-            dma((3,)),
+            dma((3 * GROUPS,)),
+            dma((3 * GROUPS,)),
             dma((CLIPS_HERE,)),
             dma((3 * OWN,)),
-            dma((6,)),
-            dma((6,)),
+            dma((7,)),
+            dma((7,)),
             dma((3,)),
             dma((3,)),
             dma((OWN,)),

time: 52.8 us -> 49.7 us (0.941)
  Pallas kernels: 50.7 us -> 47.6 us
    pallas_call x1, Pallas kernels: 50.7 us -> 47.6 us  [shards(): pl.pallas_call(kernel, out_shape=jax.ShapeDtypeStruct((TOK, HALF), BF16),...]
where the time goes in v4:
time: 49.7 us; the launch traced here: 49.5 us
  Pallas kernels  47.6 us (96%)
  local copies, waits for them, and re-layouts  1.97 us (4%)
    pallas_call x1, Pallas kernels, shards(): pl.pallas_call(kernel, out_shape=jax.ShapeDtypeStruct((TOK, HALF), BF16),...  47.6 us
    unnamed x1, local copies, waits for them, and re-layouts  1.97 us

profile of v4, /device:TPU:1, one launch (start us, length us, event | category | flops | bytes accessed | tf_op | source)
XLA Modules:
  0.0 49.5 jit_solution(11781611664931782418)
XLA Ops:
  0.0 47.6 %shard_map.118 = bf16[256,1280]{1,0:T(8,128)(2,1)} custom-call(s32[3,64]{1,0:T(4,128)} %bitcast.3, s32[128]{0:T(128)} %counts_ref.1, bf16[64,256]{1,0:T(8,128)(2,1)} %bitcast.2, bf16[64,1280]{1,0:T(8,128)(2,1)} %weight_ref.1, f32[1280]{0:T(1024)} %bias_ref.1, f32[2,1280]{1,0:T(2,128)} %block_ref.1, f32[64,2,1280]{2,1,0:T(2,128)} %time_ref.1, ...), custom_call_target="tpu_custom_call" | custom-call | tf_op jit(solution)/shard_map/pallas_call | solution.py:632
  47.6 2.0 %copy.14 = bf16[256,1280]{1,0:T(8,128)(2,1)} copy(bf16[256,1280]{1,0:T(8,128)(2,1)} %shard_map.118) | data formatting | bytes 1310720

commit v5 on v4

--- a/solution.py
+++ b/solution.py
@@ -13,12 +13,14 @@
 HEADS = 20
 HD = 128
 CIN = 64
+CLIPS = 64
 TOK = 256
 PLANE = 32
 CLIPS_HERE = 16
 UNITS = 30
 OWN = 5
 GROUPS = 8
+DIRECT = 5
 BLOCK = 80
 WIRE = 72
 EPSILON = 1e-06
@@ -37,8 +39,8 @@
 
 
 def kernel(
-    shape_ref,
-    counts_ref,
+    shape_hbm,
+    counts_hbm,
     patches_ref,
     weight_ref,
     bias_ref,
@@ -50,6 +52,8 @@
     pair_bias_hbm,
     gain_hbm,
     out_ref,
+    shape_ref,
+    counts_ref,
     query_weight,
     pair_weight,
     query_bias_ref,
@@ -65,8 +69,10 @@
     row_sums_in,
     centred,
     modulated,
+    clip_rows,
     landed,
     columns,
+    partial,
     sending,
     units,
     rows_aug,
@@ -115,6 +121,7 @@
     diagonal = (sibling[0], 1 - m)
     neighbour = (s + 2 * PLANE * (1 - 2 * x_lo), m)
     adjacent = (neighbour[0], 1 - m)
+    across = (neighbour[0] - core + other, m)
 
     def remote(src, dst, send, recv, device):
         return pltpu.make_async_remote_copy(
@@ -134,7 +141,7 @@
         return carry
 
     lax.fori_loop(0, PLANE - 1, greet, 0)
-    for device in (neighbour, adjacent, partner, diagonal, sibling):
+    for device in (neighbour, across, adjacent, partner, diagonal, sibling):
         pl.semaphore_signal(barrier, inc=1, device_id=device, device_id_type=MESH)
 
     @pl.when(chip // CLIPS_HERE != core)
@@ -155,6 +162,8 @@
     adjacent_clips = pl.ds((1 - x_lo) * PLANE + core * CLIPS_HERE, CLIPS_HERE)
 
     weight_copies = [
+        pltpu.make_async_copy(shape_hbm, shape_ref, local.at[11]),
+        pltpu.make_async_copy(counts_hbm, counts_ref, local.at[12]),
         pltpu.make_async_copy(query_weight_ref, query_weight, local.at[0]),
         pltpu.make_async_copy(pair_weight_ref, pair_weight, local.at[1]),
     ]
@@ -227,7 +236,7 @@
         )
     row_sums[CIN:, :] = jnp.broadcast_to(jnp.sum(bias_all[m], axis=1, keepdims=True), (8, HD))
 
-    pl.semaphore_wait(barrier, PLANE - 1 + 5 + jnp.where(crossing, CLIPS_HERE, 0))
+    pl.semaphore_wait(barrier, PLANE - 1 + 6 + jnp.where(crossing, CLIPS_HERE, 0))
 
     param_copies = [
         remote(patches_ref, tokens.at[core], send_p.at[0], recv_p.at[0], sibling),
@@ -236,6 +245,11 @@
         remote(block_ref, block_all.at[m], send_p.at[3], recv_p.at[3], adjacent),
         remote(time_ref.at[adjacent_clips], time_all.at[m], send_p.at[4], recv_p.at[4], adjacent),
     ]
+    sums_copy = remote(row_sums, row_sums_in, send_p.at[6], recv_p.at[6], adjacent)
+    sums_copy.start()
+    for copy in param_copies:
+        copy.start()
+
     def source_of(unit):
         return rows_ref.at[:, :, pl.ds(pl.multiple_of(unit * HD, HD), HD)]
 
@@ -259,11 +273,6 @@
     def _():
         pltpu.make_async_copy(source_of(chip), landing, recv_a.at[chip]).start()
 
-    sums_copy = remote(row_sums, row_sums_in, send_p.at[6], recv_p.at[6], adjacent)
-    sums_copy.start()
-    for copy in param_copies:
-        copy.start()
-
     depth = chip // 4
 
     def group_of(index):
@@ -280,6 +289,16 @@
 
     def passed_on(index):
         block = landed.at[1 - x_lo, group_of(index), core]
+        slot = 2 * GROUPS + index
+        return remote(block, block, send_b.at[slot], recv_b.at[slot], sibling)
+
+    def to_across(index):
+        block = landed.at[x_lo, group_of(index), core]
+        slot = 2 * GROUPS + index
+        return remote(block, block, send_b.at[slot], recv_b.at[slot], across)
+
+    def from_across(index):
+        block = landed.at[1 - x_lo, group_of(index), other]
         slot = 2 * GROUPS + index
         return remote(block, block, send_b.at[slot], recv_b.at[slot], sibling)
 
@@ -292,6 +311,8 @@
                     block = landed.at[x_lo, first + step, core]
                     pltpu.make_async_copy(block, block, recv_a.at[first + step]).wait()
                 to_neighbour(index).start()
+                if index >= DIRECT:
+                    to_across(index).start()
                 to_sibling(index).start()
 
     def modulate_half(half):
@@ -301,27 +322,20 @@
         span = pl.ds(pl.multiple_of(half * HALF, HALF), HALF)
 
         def modulate(step, carry):
-            rows = pl.multiple_of(step * BLOCK, 16)
-            index = lax.broadcasted_iota(jnp.int32, (BLOCK - CIN, HALF), 0)
+            rows = pl.multiple_of(step * CIN, CIN)
             scale = 1.0 + time_all[half, step, 1:2, :] + block_all[half, 1:2, :]
-            shift = time_all[half, step, 0:1, :] + block_all[half, 0:1, :]
             modulated[pl.ds(rows, CIN), span] = (centred[...] * scale).astype(BF16)
-            bias_scaled = bias_row * scale
-            bias_low = bias_scaled - bias_scaled.astype(BF16).astype(F32)
-            shift_low = shift - shift.astype(BF16).astype(F32)
-            extra = jnp.where(
-                index == 0,
-                bias_scaled,
-                jnp.where(
-                    index == 1,
-                    bias_low,
-                    jnp.where(index == 2, shift, jnp.where(index == 3, shift_low, 0.0)),
-                ),
-            )
-            modulated[pl.ds(pl.multiple_of(rows + CIN, 16), BLOCK - CIN), span] = extra.astype(BF16)
+            clip_rows[0, pl.ds(step, 1), :] = bias_row * scale
+            clip_rows[1, pl.ds(step, 1), :] = time_all[half, step, 0:1, :] + block_all[half, 0:1, :]
             return carry
 
         lax.fori_loop(0, CLIPS_HERE, modulate, 0)
+        for kind in range(2):
+            high = clip_rows[kind].astype(BF16)
+            low = (clip_rows[kind] - high.astype(F32)).astype(BF16)
+            base = CLIPS_HERE * (CIN + 2 * kind)
+            modulated[base : base + CLIPS_HERE, span] = high
+            modulated[base + CLIPS_HERE : base + 2 * CLIPS_HERE, span] = low
 
     hand_on(range(0, 3))
     sums_copy.wait_recv()
@@ -335,7 +349,7 @@
 
     @pl.when(owner)
     def _():
-        for index in range(GROUPS):
+        for index in range(DIRECT):
             to_neighbour(index).wait_recv()
             passed_on(index).start()
 
@@ -347,42 +361,55 @@
     def _():
         for index in range(GROUPS):
             to_sibling(index).wait_recv()
-            passed_on(index).wait_recv()
-        columns[...] = landed[...].reshape(D, HD)
-
+        columns[0] = landed[x_lo].reshape(HALF, HD)
+        here_span = pl.ds(pl.multiple_of(x_lo * HALF, HALF), HALF)
+        there_span = pl.ds(pl.multiple_of((1 - x_lo) * HALF, HALF), HALF)
+        for turn in range(4):
+            rows = slice(turn * 4 * CIN, (turn + 1) * 4 * CIN)
+            partial[rows, :] = jnp.dot(
+                modulated[rows, here_span], columns[0], preferred_element_type=F32
+            )
+        rows = slice(CLIPS_HERE * CIN, CLIPS_HERE * (CIN + 4))
+        partial[rows, :] = jnp.dot(
+            modulated[rows, here_span], columns[0], preferred_element_type=F32
+        )
+        for index in range(GROUPS):
+            if index >= DIRECT:
+                to_neighbour(index).wait_recv()
+            from_across(index).wait_recv()
+        columns[1] = landed[1 - x_lo].reshape(HALF, HD)
+        extra = partial[rows, :] + jnp.dot(
+            modulated[rows, there_span], columns[1], preferred_element_type=F32
+        )
+        bias_rows = extra[:CLIPS_HERE] + extra[CLIPS_HERE : 2 * CLIPS_HERE]
+        shift_rows = extra[2 * CLIPS_HERE : 3 * CLIPS_HERE] + extra[3 * CLIPS_HERE :]
+        bias_low = bias_rows - bias_rows.astype(BF16).astype(F32)
+        shift_low = shift_rows - shift_rows.astype(BF16).astype(F32)
+        index = lax.broadcasted_iota(jnp.int32, (BLOCK - CIN, HD), 0)
+        for target in range(CLIPS_HERE):
+            row = slice(target, target + 1)
+            tail = jnp.where(
+                index == 0,
+                bias_rows[row],
+                jnp.where(
+                    index == 1,
+                    bias_low[row],
+                    jnp.where(
+                        index == 2, shift_rows[row], jnp.where(index == 3, shift_low[row], 0.0)
+                    ),
+                ),
+            )
+            sending[target, CIN:, :] = tail.astype(BF16)
         ahead = (core * 4 - depth) % GROUPS
         backward = jnp.logical_or(ahead <= 2, ahead == 7)
         for turn in range(4):
             chunk = jnp.where(backward, 3 - turn, turn)
-            folded = jnp.dot(
-                modulated[pl.ds(pl.multiple_of(chunk * 4 * BLOCK, 4 * BLOCK), 4 * BLOCK), :],
-                columns[...],
-                preferred_element_type=F32,
+            span = pl.ds(pl.multiple_of(chunk * 4 * CIN, 4 * CIN), 4 * CIN)
+            folded = partial[span, :] + jnp.dot(
+                modulated[span, there_span], columns[1], preferred_element_type=F32
             )
             for piece in range(4):
-                target = chunk * 4 + piece
-                block = folded[piece * BLOCK : (piece + 1) * BLOCK]
-                extra = block[CIN:]
-                bias_row = extra[0:1] + extra[1:2]
-                shift_row = extra[2:3] + extra[3:4]
-                index = lax.broadcasted_iota(jnp.int32, (BLOCK - CIN, HD), 0)
-                tail = jnp.where(
-                    index == 0,
-                    bias_row,
-                    jnp.where(
-                        index == 1,
-                        bias_row - bias_row.astype(BF16).astype(F32),
-                        jnp.where(
-                            index == 2,
-                            shift_row,
-                            jnp.where(
-                                index == 3, shift_row - shift_row.astype(BF16).astype(F32), 0.0
-                            ),
-                        ),
-                    ),
-                )
-                sending[target, 0:CIN, :] = block[:CIN].astype(BF16)
-                sending[target, CIN:, :] = tail.astype(BF16)
+                sending[chunk * 4 + piece, 0:CIN, :] = folded[piece * CIN : (piece + 1) * CIN].astype(BF16)
 
             for piece in range(4):
                 target = chunk * 4 + (piece + chip // 4) % 4
@@ -556,15 +583,16 @@
 
     def attend(head, carry):
         keys = (key_rows[head] * key_acc[...]).astype(BF16)
-        for part in range(2):
-            rows = slice(part * TOK, (part + 1) * TOK)
+        for part in (other, core):
+            rows = pl.ds(pl.multiple_of(part * TOK, TOK), TOK)
             queries = (query_rows[head, rows, :] * query_acc[rows, :]).astype(BF16)
             scores = lax.dot_general(queries, keys, contract_lanes, preferred_element_type=F32)
             weights = jnp.exp2(scores).astype(BF16)
             summed = jnp.dot(weights, value_rows[head], preferred_element_type=F32)
             kept = jnp.where(valid_rows[rows, :] > 0.0, summed[:, :HD] / summed[:, HD:], 0.0)
             result[part, head] = kept.astype(BF16)
-        other_result(head).start()
+            if part is other:
+                other_result(head).start()
         own_result(head).start()
         return carry
 
@@ -626,15 +654,16 @@
     keyvalue_bias,
     norm_gain,
 ):
-    smem = pl.BlockSpec(memory_space=pltpu.SMEM)
     anywhere = pl.BlockSpec(memory_space=pl.ANY)
     dma = pltpu.SemaphoreType.DMA
     return pl.pallas_call(
         kernel,
         out_shape=jax.ShapeDtypeStruct((TOK, HALF), BF16),
-        in_specs=[smem, smem] + [anywhere] * 10,
+        in_specs=[pl.BlockSpec(memory_space=pltpu.HBM)] * 12,
         out_specs=anywhere,
         scratch_shapes=[
+            pltpu.SMEM((3, CLIPS), jnp.int32),
+            pltpu.SMEM((2 * CLIPS,), jnp.int32),
             pltpu.VMEM((20, HALF), BF16),
             pltpu.VMEM((20, D), BF16),
             pltpu.VMEM((1, HALF), F32),
@@ -649,9 +678,11 @@
             pltpu.VMEM((CIN + 8, HD), F32),
             pltpu.VMEM((CIN + 8, HD), F32),
             pltpu.VMEM((CIN, HALF), F32),
-            pltpu.VMEM((CLIPS_HERE * BLOCK, D), BF16),
+            pltpu.VMEM((CLIPS_HERE * (CIN + 4), D), BF16),
+            pltpu.VMEM((2, CLIPS_HERE, HALF), F32),
             pltpu.VMEM((2, PLANE, 2, 5, 4, HD), BF16),
-            pltpu.VMEM((D, HD), BF16),
+            pltpu.VMEM((2, HALF, HD), BF16),
+            pltpu.VMEM((CLIPS_HERE * (CIN + 4), HD), F32),
             pltpu.VMEM((CLIPS_HERE, BLOCK, HD), BF16),
             pltpu.VMEM((3 * OWN, HD, HD), BF16),
             pltpu.VMEM((2 * TOK, HD), BF16),
@@ -679,25 +710,30 @@
             dma((3,)),
             dma((OWN,)),
             dma((OWN,)),
-            dma((11,)),
+            dma((13,)),
             dma((OWN,)),
         ],
         compiler_params=pltpu.CompilerParams(
-            collective_id=0, has_side_effects=True, vmem_limit_bytes=60 << 20
+            collective_id=0, has_side_effects=True, vmem_limit_bytes=24 << 20
         ),
     )(
-        clip_shape.T,
-        shard_counts,
-        patches.T,
-        patch_weight,
-        patch_bias,
-        block_mod,
-        time_mod,
-        w_query,
-        w_keyvalue,
-        query_bias,
-        keyvalue_bias,
-        norm_gain,
+        *[
+            pltpu.with_memory_space_constraint(value, pltpu.HBM)
+            for value in (
+                clip_shape.T,
+                shard_counts,
+                patches.T,
+                patch_weight,
+                patch_bias,
+                block_mod,
+                time_mod,
+                w_query,
+                w_keyvalue,
+                query_bias,
+                keyvalue_bias,
+                norm_gain,
+            )
+        ]
     )
 
 

time: 49.7 us -> 47.8 us (0.962)
  local copies, waits for them, and re-layouts: 1.97 us -> 0.84 us
  Pallas kernels: 47.6 us -> 46.8 us
    unnamed x1, local copies, waits for them, and re-layouts: 1.97 us -> 0.84 us
    pallas_call x1, Pallas kernels: 47.6 us -> 46.8 us  [shards(): pl.pallas_call(kernel, out_shape=jax.ShapeDtypeStruct((TOK, HALF), BF16),...]
where the time goes in v5:
time: 47.8 us; the launch traced here: 47.7 us
  Pallas kernels  46.8 us (98%)
  local copies, waits for them, and re-layouts  0.84 us (2%)
    pallas_call x1, Pallas kernels, shards(): pl.pallas_call(kernel, out_shape=jax.ShapeDtypeStruct((TOK, HALF), BF16),...  46.8 us

profile of v5, /device:TPU:1, one launch (start us, length us, event | category | flops | bytes accessed | tf_op | source)
XLA Modules:
  0.0 47.7 jit_solution(396691932999967599)
XLA Ops:
  0.0 46.8 %shard_map.118 = bf16[256,1280]{1,0:T(8,128)(2,1)S(1)} custom-call(s32[3,64]{1,0:T(4,128)} %bitcast.3, s32[128]{0:T(128)} %counts_hbm.1, bf16[64,256]{1,0:T(8,128)(2,1)} %bitcast.2, bf16[64,1280]{1,0:T(8,128)(2,1)} %weight_ref.1, f32[1280]{0:T(1024)} %bias_ref.1, f32[2,1280]{1,0:T(2,128)} %block_ref.1, f32[64,2,1280]{2,1,0:T(2,128)} %time_ref.1, ...), custom_call_target="tpu_custom_call" | custom-call | tf_op jit(solution)/shard_map/pallas_call | solution.py:659
  46.8 0.8 %copy.14 = bf16[256,1280]{1,0:T(8,128)(2,1)} copy(bf16[256,1280]{1,0:T(8,128)(2,1)S(1)} %shard_map.118) | data formatting | bytes 1310720
